TPU v7x, 512 devices: a whole 4x8x8 slice. The times are simulated.
512 devices in a mesh: seq: 64 (over z, x, core), head: 8 (over y).
Axes of the slice: x: 4, y: 8, z: 8, core: 2. Of those that a mesh axis runs over, the one named last changes fastest.
Arguments:
- query_rows: bfloat16 [8192, 8192], P('seq', 'head'), may hold values from -6 to 6
- key_rows: bfloat16 [8192, 8192], P('seq', 'head'), may hold values from -6 to 6
- value_rows: bfloat16 [8192, 8192], P('seq', 'head'), may hold values from -6 to 6
- grad_output: bfloat16 [8192, 8192], P('seq', 'head'), may hold values from -6 to 6
- norm_gain: float32 [8192], P('head'), may hold values from 0.5 to 1.5
Outputs:
- grad_query: bfloat16 [8192, 8192], P('seq', 'head')
- grad_key: bfloat16 [8192, 8192], P('seq', 'head')
- grad_value: bfloat16 [8192, 8192], P('seq', 'head')
- grad_gain: float32 [8192], P('head')
All inputs are finite; a program needn't handle non-finite values.
Results may differ from a plain program's by a relative error of at most 0.0031.
Values sent between devices are 32-bit elements; how exact they have to be, the bound alone decides.
No kernel may reach another device: no remote copies, remote signals or barrier semaphores. Data moves between devices by JAX's collectives and lax.ppermute only.
A program may use at most 128 MiB of HBM per device.

v0:
```python
import jax
import jax.numpy as jnp
from jax import lax
from jax.sharding import PartitionSpec as P

DH = 128
W = 8192


epsilon = 1e-06
highest = lax.Precision.HIGHEST


def order_weights(blocks, earlier):
    rows = lax.broadcasted_iota(jnp.int32, (blocks, blocks), 0)
    cols = lax.broadcasted_iota(jnp.int32, (blocks, blocks), 1)
    if earlier:
        return (cols < rows).astype(jnp.float32)
    return (cols > rows).astype(jnp.float32)


def shards(query_rows, key_rows, value_rows, grad_output, norm_gain):
    count = query_rows.shape[0]
    local_width = query_rows.shape[1]
    local_heads = local_width // DH
    blocks = lax.axis_size("seq")
    query_heads = query_rows.reshape(count, local_heads, DH)
    key_heads = key_rows.reshape(count, local_heads, DH)
    value_heads = value_rows.reshape(count, local_heads, DH)
    upper = lax.broadcasted_iota(jnp.int32, (count, count), 0)
    lower = lax.broadcasted_iota(jnp.int32, (count, count), 1)
    causal = (upper >= lower)[None]
    block_state = jnp.einsum(
        "thd,the->hde", key_heads, value_heads, preferred_element_type=jnp.float32
    )
    share_rows = block_state.reshape(blocks, -1)
    mine = lax.all_to_all(share_rows, "seq", split_axis=0, concat_axis=0, tiled=True)
    summed = jnp.dot(order_weights(blocks, True), mine, precision=highest)
    back = lax.all_to_all(summed, "seq", split_axis=0, concat_axis=0, tiled=True)
    prior = back.reshape(block_state.shape)
    scores = jnp.einsum("thd,shd->hts", query_heads, key_heads, preferred_element_type=jnp.float32)
    probs = jnp.where(causal, scores, 0.0).astype(jnp.bfloat16)
    attn = jnp.einsum("hts,she->the", probs, value_heads, preferred_element_type=jnp.float32)
    attn = attn + jnp.einsum(
        "thd,hde->the", query_heads.astype(jnp.float32), prior, precision=highest
    )
    flat = attn.reshape(count, local_width)
    grad_float = grad_output.astype(jnp.float32)
    scaled = grad_float * norm_gain[None, :]
    square_part = jnp.sum(flat * flat, axis=1)
    square = lax.psum(square_part, "head")
    inverse = lax.rsqrt(square / W + epsilon)
    normed = flat * inverse[:, None]
    cross = lax.psum(jnp.sum(scaled * normed, axis=1), "head")
    grad_attn = inverse[:, None] * (scaled - normed * (cross / W)[:, None])
    grad_gain = lax.psum(jnp.sum(grad_float * normed, axis=0), "seq")
    grad_heads = grad_attn.reshape(count, local_heads, DH)
    block_grad = jnp.einsum(
        "thd,the->hde", query_heads.astype(jnp.float32), grad_heads, precision=highest
    )
    grad_share_rows = block_grad.reshape(blocks, -1)
    grad_mine = lax.all_to_all(grad_share_rows, "seq", split_axis=0, concat_axis=0, tiled=True)
    grad_summed = jnp.dot(order_weights(blocks, False), grad_mine, precision=highest)
    grad_back = lax.all_to_all(grad_summed, "seq", split_axis=0, concat_axis=0, tiled=True)
    later = grad_back.reshape(block_grad.shape)
    grad_round = grad_heads.astype(jnp.bfloat16)
    dprobs = jnp.einsum("the,she->hts", grad_round, value_heads, preferred_element_type=jnp.float32)
    dprobs = jnp.where(causal, dprobs, 0.0).astype(jnp.bfloat16)
    grad_query = jnp.einsum("hts,shd->thd", dprobs, key_heads, preferred_element_type=jnp.float32)
    grad_query = grad_query + jnp.einsum("the,hde->thd", grad_heads, prior, precision=highest)
    grad_key = jnp.einsum("hts,thd->shd", dprobs, query_heads, preferred_element_type=jnp.float32)
    grad_key = grad_key + jnp.einsum(
        "she,hde->shd", value_heads.astype(jnp.float32), later, precision=highest
    )
    grad_value = jnp.einsum("hts,the->she", probs, grad_round, preferred_element_type=jnp.float32)
    grad_value = grad_value + jnp.einsum(
        "shd,hde->she", key_heads.astype(jnp.float32), later, precision=highest
    )
    return (
        grad_query.astype(jnp.bfloat16).reshape(count, local_width),
        grad_key.astype(jnp.bfloat16).reshape(count, local_width),
        grad_value.astype(jnp.bfloat16).reshape(count, local_width),
        grad_gain,
    )


def solution(mesh):
    placed = (P("seq", "head"), P("seq", "head"), P("seq", "head"), P("seq", "head"), P("head"))
    return jax.shard_map(
        shards,
        mesh=mesh,
        in_specs=placed,
        out_specs=(P("seq", "head"), P("seq", "head"), P("seq", "head"), P("head")),
        check_vma=False,
    )
```

profile of v0, /device:TPU:1, one launch (start us, length us, event | category | flops | bytes accessed | tf_op | source)
XLA Modules:
  0.0 260.9 jit_solution(1061433663784870662)
XLA Ops:
  0.6 1.0 copy.117
  2.1 32.3 %all_to_all.42 = f32[64,1,2048]{2,1,0:T(1,128)S(1)} all-to-all(f32[64,1,2048]{2,1,0:T(1,128)S(1)} %bitcast.127), channel_id=1, replica_groups=mesh['seq'=64,'head'=8] {'seq'}, dimensions={0} | all-to-all | bytes 1048576 | tf_op jit(solution)/shard_map/all_to_all | solution.py:37
  34.5 0.6 convolution_bitcast_fusion.1
  35.0 1.3 copy.87
  36.4 5.8 %all-to-all-start.1 = ((f32[64,1,2048]{2,1,0:T(1,128)}), f32[64,1,2048]{2,1,0:T(1,128)S(1)}, u32[]{:S(2)}, u32[]{:S(2)}) async-start(f32[64,1,2048]{2,1,0:T(1,128)} %copy.87), calls=%async_computation.1 | async-start | bytes 1048576 | tf_op jit(solution)/shard_map/all_to_all | solution.py:39
  42.6 17.3 %all-to-all-done.1 = f32[64,1,2048]{2,1,0:T(1,128)S(1)} async-done(((f32[64,1,2048]{2,1,0:T(1,128)}), f32[64,1,2048]{2,1,0:T(1,128)S(1)}, u32[]{:S(2)}, u32[]{:S(2)}) %all-to-all-start.1) | async-done | bytes 524320 | tf_op jit(solution)/shard_map/all_to_all | solution.py:39
  59.9 0.6 convolution_bitcast_fusion.6
  60.5 0.4 multiply_reduce_fusion
  60.8 14.2 %psum.21 = f32[128]{0:T(128)S(1)} all-reduce(f32[128]{0:T(128)S(1)} %get-tuple-element.22), channel_id=1, replica_groups=mesh['seq'=64,'head'=8] {'head'}, use_global_device_ids=true, to_apply=%region_1.2 | all-reduce | flops 128 | bytes 1024 | tf_op jit(solution)/shard_map/psum | solution.py:51
  75.2 0.7 copy-done.3
  76.2 11.1 %psum.22 = f32[128]{0:T(128)S(1)} all-reduce(f32[128]{0:T(128)S(1)} %get-tuple-element.21), channel_id=1, replica_groups=mesh['seq'=64,'head'=8] {'head'}, use_global_device_ids=true, to_apply=%region_3.4 | all-reduce | flops 128 | bytes 1024 | tf_op jit(solution)/shard_map/psum | solution.py:54
  87.7 0.4 convolution_bitcast_fusion.4
  88.3 30.4 %all_to_all.43 = f32[64,1,2048]{2,1,0:T(1,128)S(1)} all-to-all(f32[64,1,2048]{2,1,0:T(1,128)S(1)} %bitcast.126), channel_id=1, replica_groups=mesh['seq'=64,'head'=8] {'seq'}, dimensions={0} | all-to-all | bytes 1048576 | tf_op jit(solution)/shard_map/all_to_all | solution.py:62
  118.8 0.6 convolution_bitcast_fusion
  119.3 1.3 copy.101
  120.7 5.7 %all-to-all-start.3 = ((f32[64,1,2048]{2,1,0:T(1,128)}), f32[64,1,2048]{2,1,0:T(1,128)S(1)}, u32[]{:S(2)}, u32[]{:S(2)}) async-start(f32[64,1,2048]{2,1,0:T(1,128)} %copy.101), calls=%async_computation.3 | async-start | bytes 1048576 | tf_op jit(solution)/shard_map/all_to_all | solution.py:64
  126.4 0.3 fusion.4
  126.7 0.6 convolution_bitcast_fusion.8
  127.7 0.9 copy.105
  128.5 128.6 %psum.23 = f32[1024]{0:T(1024)} all-reduce(f32[1024]{0:T(1024)S(1)} %get-tuple-element.20), channel_id=1, replica_groups=mesh['seq'=64,'head'=8] {'seq'}, use_global_device_ids=true, to_apply=%region_5.6 | all-reduce | flops 1024 | bytes 8192 | tf_op jit(solution)/shard_map/psum | solution.py:56
  257.1 0.6 fusion.22
  257.7 0.7 convolution_bitcast_fusion.3
  258.9 0.9 copy.107
  260.0 0.9 copy.106
  (28 shorter events, 2.9 us)
Async XLA Ops:
  0.6 1.3 copy-start
  36.4 5.9 %copy-start.1 = (bf16[128,1024]{1,0:T(8,128)(2,1)S(1)}, bf16[128,1024]{1,0:T(8,128)(2,1)}, u32[]{:S(2)}) copy-start(bf16[128,1024]{1,0:T(8,128)(2,1)} %param.5) | copy-start | bytes 786436
  36.4 5.9 %copy-start.2 = (bf16[128,1024]{1,0:T(8,128)(2,1)S(1)}, bf16[128,1024]{1,0:T(8,128)(2,1)}, u32[]{:S(2)}) copy-start(bf16[128,1024]{1,0:T(8,128)(2,1)} %param.6) | copy-start | bytes 786436
  36.4 23.5 %all-to-all-start.1 = ((f32[64,1,2048]{2,1,0:T(1,128)}), f32[64,1,2048]{2,1,0:T(1,128)S(1)}, u32[]{:S(2)}, u32[]{:S(2)}) async-start(f32[64,1,2048]{2,1,0:T(1,128)} %copy.87), calls=%async_computation.1 | async-start | bytes 1048576 | tf_op jit(solution)/shard_map/all_to_all | solution.py:39
  42.5 17.9 %copy-start.4 = (bf16[8,128,128]{2,1,0:T(8,128)(2,1)}, bf16[8,128,128]{2,1,0:T(8,128)(2,1)S(1)}, u32[]{:S(2)}) copy-start(bf16[8,128,128]{2,1,0:T(8,128)(2,1)S(1)} %fusion.3) | copy-start | bytes 786436
  75.0 1.0 copy-start.3
  75.0 1.0 copy-start.6
  120.7 136.4 %all-to-all-start.3 = ((f32[64,1,2048]{2,1,0:T(1,128)}), f32[64,1,2048]{2,1,0:T(1,128)S(1)}, u32[]{:S(2)}, u32[]{:S(2)}) async-start(f32[64,1,2048]{2,1,0:T(1,128)} %copy.101), calls=%async_computation.3 | async-start | bytes 1048576 | tf_op jit(solution)/shard_map/all_to_all | solution.py:64
  257.7 1.0 copy-start.5
where the time goes:
time: 262 us; the launch traced here: 261 us
  blocking collectives  217 us (83%)
  waiting for transfers between devices  17.3 us (7%)
  starting transfers between devices  11.5 us (4%)
  local copies, waits for them, and re-layouts  8.1 us (3%)
  matrix products  5.98 us (2%)
    psum x1, blocking collectives, shards(): grad_gain = lax.psum(jnp.sum(grad_float * normed, axis=0), 'seq')  129 us
    all_to_all x1, blocking collectives, shards(): lax.all_to_all(share_rows, 'seq', split_axis=0, concat_axis=0, tiled=True)  32.3 us
    all_to_all x1, blocking collectives, shards(): lax.all_to_all(grad_share_rows, 'seq', split_axis=0, concat_axis=0, tiled...  30.4 us
    all_to_all x1, waiting for transfers between devices, shards(): lax.all_to_all(summed, 'seq', split_axis=0, concat_axis=0, tiled=True)  17.3 us
    psum x1, blocking collectives, shards(): square = lax.psum(square_part, 'head')  14.2 us
    psum x1, blocking collectives, shards(): cross = lax.psum(jnp.sum(scaled * normed, axis=1), 'head')  11.1 us
    all_to_all x1, starting transfers between devices, shards(): lax.all_to_all(summed, 'seq', split_axis=0, concat_axis=0, tiled=True)  5.82 us
    all_to_all x1, starting transfers between devices, shards(): lax.all_to_all(grad_summed, 'seq', split_axis=0, concat_axis=0, tiled=True)  5.69 us
  transfers between devices with their start and end apart: 2, of which 1 were waited for; matrix products, arithmetic and copies ran while one was open for 1% of the time, Pallas kernels for 0%

commit v1 on v0

v1 whole, which is shorter than its diff:
```python
import functools

import jax
import jax.numpy as jnp
from jax import lax
from jax.experimental import pallas as pl
from jax.experimental.pallas import tpu as pltpu
from jax.sharding import Mesh, PartitionSpec as P

DH = 128
EPS = 1e-06
F32 = jnp.float32
BF16 = jnp.bfloat16


def dot(a, b, ca, cb):
    return lax.dot_general(a, b, (((ca,), (cb,)), ((), ())), preferred_element_type=F32)


def split(x):
    hi = x.astype(BF16)
    return hi, (x - hi.astype(F32)).astype(BF16)


def causal():
    rows = lax.broadcasted_iota(jnp.int32, (DH, DH), 0)
    cols = lax.broadcasted_iota(jnp.int32, (DH, DH), 1)
    return rows >= cols


def hs(h):
    return slice(h * DH, (h + 1) * DH)


def whole(shape):
    return pl.BlockSpec(shape, lambda i, c: (0,) * len(shape))


def call(name, body, core, ins, in_specs, outs, out_specs=None, scratch=()):
    if out_specs is None:
        out_specs = [whole(o.shape) for o in outs]
    return pl.pallas_call(
        body,
        name=name,
        out_shape=outs,
        grid_spec=pltpu.PrefetchScalarGridSpec(
            num_scalar_prefetch=1,
            grid=(1,),
            in_specs=in_specs,
            out_specs=out_specs,
            scratch_shapes=list(scratch),
        ),
    )(core, *ins)


def sds(shape, dtype):
    return jax.ShapeDtypeStruct(shape, dtype)


def send_body(c, q, k, v, g, out):
    for i, ref in enumerate((q, k, v, g)):
        out[i] = ref[...].astype(F32)


def state_body(c, q, k, v, g, got, rows, first, total):
    mine = pl.multiple_of(c[0] * DH, DH)
    other = pl.multiple_of((1 - c[0]) * DH, DH)
    for i, ref in enumerate((q, k, v, g)):
        rows[i, pl.ds(mine, DH), :] = ref[...]
        rows[i, pl.ds(other, DH), :] = got[i].astype(BF16)
    for h in range(first.shape[0]):
        s0 = dot(rows[1, 0:DH, hs(h)], rows[2, 0:DH, hs(h)], 0, 0)
        s1 = dot(rows[1, DH : 2 * DH, hs(h)], rows[2, DH : 2 * DH, hs(h)], 0, 0)
        first[h] = s0
        total[hs(h), :] = s0 + s1


def local_body(c, rows, probs, intra):
    mask = causal()
    heads = probs.shape[1]
    for b in range(2):
        r = slice(b * DH, (b + 1) * DH)
        for h in range(heads):
            p = dot(rows[0, r, hs(h)], rows[1, r, hs(h)], 1, 1)
            p = jnp.where(mask, p, 0.0).astype(BF16)
            probs[b, h] = p
            intra[r, hs(h)] = dot(p, rows[2, r, hs(h)], 1, 0)


def earlier_body(n, c, x, out):
    share = x.shape[0] // n
    acc = jnp.zeros((share, DH), F32)
    for i in range(n):
        out[i * share : (i + 1) * share, :] = acc
        if i + 1 < n:
            acc = acc + x[i * share : (i + 1) * share, :]


def attn_body(c, rows, intra, first, prior, gain, flat, parts):
    heads = first.shape[0]
    for b in range(2):
        r = slice(b * DH, (b + 1) * DH)
        square = jnp.zeros((DH, DH), F32)
        cross = jnp.zeros((DH, DH), F32)
        for h in range(heads):
            p = prior[hs(h), :]
            if b == 1:
                p = p + first[h]
            hi, lo = split(p)
            q = rows[0, r, hs(h)]
            f = intra[r, hs(h)] + (dot(q, lo, 1, 0) + dot(q, hi, 1, 0))
            flat[r, hs(h)] = f
            square = square + f * f
            cross = cross + (rows[3, r, hs(h)].astype(F32) * gain[:, hs(h)]) * f
        sq = jnp.sum(square.T, axis=0, keepdims=True)
        cr = jnp.sum(cross.T, axis=0, keepdims=True)
        for j in range(parts.shape[0]):
            parts[j, b : b + 1, :] = sq
            parts[j, 2 + b : 3 + b, :] = cr


def grad_body(n, width, c, rows, flat, gain, parts, gd, second, out):
    heads = second.shape[0]
    own = heads * DH // n
    total = jnp.sum(parts[...], axis=0)
    gain_rows = [jnp.zeros((1, DH), F32) for _ in range(heads)]
    sums = [None] * heads
    for b in range(2):
        r = slice(b * DH, (b + 1) * DH)
        inverse = lax.rsqrt(total[b : b + 1, :] / width + EPS)
        scale = inverse * total[2 + b : 3 + b, :] / width
        inverse = jnp.broadcast_to(inverse, (DH, DH)).T
        scale = jnp.broadcast_to(scale, (DH, DH)).T
        for h in range(heads):
            g = rows[3, r, hs(h)].astype(F32)
            normed = flat[r, hs(h)] * inverse
            d = inverse * (g * gain[:, hs(h)] - normed * scale)
            gd[r, hs(h)] = d
            gain_rows[h] = gain_rows[h] + jnp.sum(g * normed, axis=0, keepdims=True)
            hi, lo = split(d)
            q = rows[0, r, hs(h)]
            s = dot(q, lo, 0, 0) + dot(q, hi, 0, 0)
            if b == 1:
                second[h] = s
                sums[h] = sums[h] + s
            else:
                sums[h] = s
    for j in range(n):
        h, at = divmod(j * own, DH)
        out[j * (own + 1) : j * (own + 1) + own, :] = sums[h][at : at + own, :]
        out[j * (own + 1) + own : (j + 1) * (own + 1), :] = gain_rows[j % heads]


def query_body(c, rows, probs, gd, prior, first, gq, gk, gv):
    mask = causal()
    heads = first.shape[0]
    for b in range(2):
        r = slice(b * DH, (b + 1) * DH)
        for h in range(heads):
            q, k, v = rows[0, r, hs(h)], rows[1, r, hs(h)], rows[2, r, hs(h)]
            hi, lo = split(gd[r, hs(h)])
            dp = dot(hi, v, 1, 1)
            dp = jnp.where(mask, dp, 0.0).astype(BF16)
            p = prior[hs(h), :]
            if b == 1:
                p = p + first[h]
            phi, plo = split(p)
            t = dot(lo, phi, 1, 1) + dot(hi, plo, 1, 1) + dot(hi, phi, 1, 1)
            gq[r, hs(h)] = dot(dp, k, 1, 0) + t
            gk[r, hs(h)] = dot(dp, q, 0, 0)
            gv[r, hs(h)] = dot(probs[b, h], hi, 0, 0)


def later_body(n, c, x, out):
    share = x.shape[0] // n
    own = share - 1
    acc = jnp.zeros((own, DH), F32)
    gain = jnp.zeros((1, DH), F32)
    for i in range(n):
        gain = gain + x[i * share + own : (i + 1) * share, :]
    for i in reversed(range(n)):
        out[i * share : i * share + own, :] = acc
        out[i * share + own : (i + 1) * share, :] = gain
        if i:
            acc = acc + x[i * share : i * share + own, :]


def key_body(n, c, rows, gq, gk, gv, second, got, keep, send, later):
    heads = second.shape[0]
    own = heads * DH // n
    for j in range(n):
        later[j * own : (j + 1) * own, :] = got[j * (own + 1) : j * (own + 1) + own, :]
    mine = pl.multiple_of(c[0] * DH, DH)
    other = pl.multiple_of((1 - c[0]) * DH, DH)
    keep[0] = gq[pl.ds(mine, DH), :]
    send[0:DH, :] = gq[pl.ds(other, DH), :]
    for h in range(heads):
        send[3 * DH : 3 * DH + 8, hs(h)] = jnp.broadcast_to(
            got[h * (own + 1) + own : (h + 1) * (own + 1), :], (8, DH)
        )
        one = later[hs(h), :]
        zero_hi, zero_lo = split(one + second[h])
        one_hi, one_lo = split(one)

        def put(b, kept, sent, hi, lo):
            r = slice(b * DH, (b + 1) * DH)
            k, v = rows[1, r, hs(h)], rows[2, r, hs(h)]
            dk = gk[r, hs(h)] + (dot(v, lo, 1, 1) + dot(v, hi, 1, 1))
            dv = gv[r, hs(h)] + (dot(k, lo, 1, 0) + dot(k, hi, 1, 0))
            if kept is not None:
                kept[1, :, hs(h)] = dk
                kept[2, :, hs(h)] = dv
            else:
                sent[DH : 2 * DH, hs(h)] = dk
                sent[2 * DH : 3 * DH, hs(h)] = dv

        @pl.when(c[0] == 0)
        def _():
            put(0, keep, None, zero_hi, zero_lo)
            put(1, None, send, one_hi, one_lo)

        @pl.when(c[0] == 1)
        def _():
            put(0, None, send, zero_hi, zero_lo)
            put(1, keep, None, one_hi, one_lo)


def final_body(c, keep, gain_keep, got, gq, gk, gv, gain):
    half = keep.shape[2]

    def put(at, away):
        for i, ref in enumerate((gq, gk, gv)):
            ref[:, at : at + half] = keep[i].astype(BF16)
            ref[:, away : away + half] = got[i * DH : (i + 1) * DH, :].astype(BF16)
        gain[:, at : at + half] = gain_keep[0:1, :]
        gain[:, away : away + half] = got[3 * DH : 3 * DH + 1, :]

    @pl.when(c[0] == 0)
    def _():
        put(0, half)

    @pl.when(c[0] == 1)
    def _():
        put(half, 0)


def shards(query_rows, key_rows, value_rows, grad_output, norm_gain):
    count, width = query_rows.shape
    half = width // 2
    heads = half // DH
    both = 2 * count
    chips = lax.axis_size("chip")
    columns = lax.axis_size("head")
    full = columns * width
    at = lax.axis_index("core")
    core = at.astype(jnp.int32).reshape(1)
    swap = [(0, 1), (1, 0)]
    args = (query_rows, key_rows, value_rows, grad_output)
    gains = norm_gain.reshape(1, width)
    mine = pl.BlockSpec((count, half), lambda i, c: (0, c[0]))
    away = pl.BlockSpec((count, half), lambda i, c: (0, 1 - c[0]))
    my_gain = pl.BlockSpec((1, half), lambda i, c: (0, c[0]))
    rows_s = sds((4, both, half), BF16)
    act = sds((both, half), F32)
    state = sds((heads, DH, DH), F32)
    flat_state = sds((heads * DH, DH), F32)
    padded = sds((heads * DH + chips, DH), F32)
    w_rows, w_act, w_state = whole(rows_s.shape), whole(act.shape), whole(state.shape)
    w_flat, w_pad = whole(flat_state.shape), whole(padded.shape)

    def exchange(x):
        y = lax.all_to_all(
            x.reshape(chips, 1, -1), "chip", split_axis=0, concat_axis=0, tiled=True
        )
        return y.reshape(x.shape)

    sent = call("send", send_body, core, args, [away] * 4, [sds((4, count, half), F32)])[0]
    got = lax.ppermute(sent, "core", swap)
    rows, first, total = call(
        "state", state_body, core, (*args, got), [mine] * 4 + [whole(got.shape)],
        [rows_s, state, flat_state],
    )
    mine_states = exchange(total)
    probs, intra = call(
        "local", local_body, core, (rows,), [w_rows],
        [sds((2, heads, DH, DH), BF16), act],
    )
    sums = call(
        "earlier", functools.partial(earlier_body, chips), core, (mine_states,), [w_flat],
        [flat_state],
    )[0]
    prior = exchange(sums)
    group = 2 * columns
    flat, parts = call(
        "attn", attn_body, core, (rows, intra, first, prior, gains),
        [w_rows, w_act, w_state, w_flat, my_gain],
        [act, sds((group, 4, DH), F32)],
    )
    parts = lax.all_to_all(parts, ("core", "head"), split_axis=0, concat_axis=0, tiled=True)
    gd, second, block = call(
        "grad", functools.partial(grad_body, chips, full), core,
        (rows, flat, gains, parts),
        [w_rows, w_act, my_gain, whole(parts.shape)],
        [act, state, padded],
    )
    mine_grads = exchange(block)
    gq, gk, gv = call(
        "query", query_body, core, (rows, probs, gd, prior, first),
        [w_rows, whole(probs.shape), w_act, w_flat, w_state],
        [act, act, act],
    )
    later_sums = call(
        "later", functools.partial(later_body, chips), core, (mine_grads,), [w_pad], [padded]
    )[0]
    later = exchange(later_sums)
    keep, send = call(
        "key", functools.partial(key_body, chips), core,
        (rows, gq, gk, gv, second, later),
        [w_rows, w_act, w_act, w_act, w_state, w_pad],
        [sds((3, count, half), F32), sds((3 * count + 8, half), F32)],
        scratch=[pltpu.VMEM(flat_state.shape, F32)],
    )
    back = lax.ppermute(send, "core", swap)
    outs = [sds((count, width), BF16)] * 3 + [sds((1, width), F32)]
    tail = pl.BlockSpec((8, half), lambda i, c: (3 * count // 8, 0))
    gq, gk, gv, gain = call(
        "final", final_body, core, (keep, send, back),
        [whole(keep.shape), tail, whole(back.shape)], outs,
    )
    return gq, gk, gv, gain.reshape(width)


def solution(mesh):
    names = dict(mesh.shape)
    inner = Mesh(
        mesh.devices.reshape(names["seq"] // 2, 2, names["head"]), ("chip", "core", "head")
    )
    seq = ("chip", "core")
    placed = (P(seq, "head"),) * 4 + (P("head"),)
    return jax.shard_map(
        shards,
        mesh=inner,
        in_specs=placed,
        out_specs=(P(seq, "head"),) * 3 + (P("head"),),
        check_vma=False,
    )
```

time: 262 us -> 127 us (0.48)
  blocking collectives: 217 us -> 53.1 us
  Pallas kernels: 0 us -> 28.2 us
  starting transfers between devices: 11.5 us -> 23.7 us
  matrix products: 5.98 us -> 0 us
  local copies, waits for them, and re-layouts: 8.1 us -> 3.3 us
    psum x3 -> x0, blocking collectives: 154 us -> none  [the longest x1 129 us: shards(): grad_gain = lax.psum(jnp.sum(grad_float * normed, axis=0), 'seq')]
    pallas_call x0 -> x10, Pallas kernels: none -> 28.2 us  [call(): pl.pallas_call(body, name=name, out_shape=outs, grid_spec=pltpu.PrefetchS...]
    ppermute x0 -> x2, starting transfers between devices: none -> 14.5 us  [the longest x1 8.73 us: shards(): got = lax.ppermute(sent, 'core', swap)]
    all_to_all x2 -> x3, blocking collectives: 62.8 us -> 53.1 us  [the longest x2 35.5 us: exchange(): lax.all_to_all(x.reshape(chips, 1, -1), 'chip', split_axis=0, concat_axis...]
    dot_general x14 -> x0, matrix products: 5.98 us -> none  [the longest x1 0.66 us: shards(): jnp.einsum('she,hde->shd', value_heads.astype(jnp.float32), later, precis...]
    ppermute x0 -> x2, waiting for transfers between devices: none -> 4.6 us  [the longest x1 2.48 us: shards(): got = lax.ppermute(sent, 'core', swap)]
    all_to_all x2, waiting for transfers between devices: 17.3 us -> 13.1 us  [exchange(): lax.all_to_all(x.reshape(chips, 1, -1), 'chip', split_axis=0, concat_axis...]
    all_to_all x2 -> x0, local copies, waits for them, and re-layouts: 2.66 us -> none  [the longest x1 1.33 us: shards(): lax.all_to_all(summed, 'seq', split_axis=0, concat_axis=0, tiled=True)]
  transfers between devices with their start and end apart: 2 -> 4, of which waited for: 1 -> 4; matrix products, arithmetic and copies ran while one was open for 1% -> 0% of each run, Pallas kernels for 0% -> 6%
where the time goes in v1:
time: 127 us
  blocking collectives  53.1 us (42%)
  Pallas kernels  28.2 us (22%)
  starting transfers between devices  23.7 us (19%)
  waiting for transfers between devices  17.7 us (14%)
  local copies, waits for them, and re-layouts  3.3 us (3%)
    all_to_all x2, blocking collectives, exchange(): lax.all_to_all(x.reshape(chips, 1, -1), 'chip', split_axis=0, concat_axis...  35.5 us
    pallas_call x10, Pallas kernels, call(): pl.pallas_call(body, name=name, out_shape=outs, grid_spec=pltpu.PrefetchS...  28.2 us
    all_to_all x1, blocking collectives, shards(): lax.all_to_all(parts, ('core', 'head'), split_axis=0, concat_axis=0, tile...  17.5 us
    all_to_all x2, waiting for transfers between devices, exchange(): lax.all_to_all(x.reshape(chips, 1, -1), 'chip', split_axis=0, concat_axis...  13.1 us
    all_to_all x2, starting transfers between devices, exchange(): lax.all_to_all(x.reshape(chips, 1, -1), 'chip', split_axis=0, concat_axis...  9.24 us
    ppermute x1, starting transfers between devices, shards(): got = lax.ppermute(sent, 'core', swap)  8.73 us
    ppermute x1, starting transfers between devices, shards(): back = lax.ppermute(send, 'core', swap)  5.77 us
    unnamed x8, local copies, waits for them, and re-layouts  3.3 us
  transfers between devices with their start and end apart: 4, of which 4 were waited for; matrix products, arithmetic and copies ran while one was open for 0% of the time, Pallas kernels for 6%

profile of v1, /device:TPU:1, one launch (start us, length us, event | category | flops | bytes accessed | tf_op | source)
XLA Modules:
  0.0 126.6 jit_solution(7905773546344292518)
XLA Ops:
  0.6 2.1 %send.1 = f32[4,128,512]{2,1,0:T(8,128)} custom-call(s32[1]{0:T(128)} %bitcast.c, bf16[128,1024]{1,0:T(8,128)(2,1)} %q.3, bf16[128,1024]{1,0:T(8,128)(2,1)} %k.3, bf16[128,1024]{1,0:T(8,128)(2,1)} %v.3, bf16[128,1024]{1,0:T(8,128)(2,1)} %g.3), custom_call_target="tpu_custom_call" | custom-call | tf_op jit(solution)/shard_map/send/pallas_call | solution.py:42
  2.8 8.7 %collective-permute-start = (f32[4,128,512]{2,1,0:T(8,128)}, f32[4,128,512]{2,1,0:T(8,128)S(1)}, u32[]{:S(2)}, u32[]{:S(2)}) collective-permute-start(f32[4,128,512]{2,1,0:T(8,128)} %send.1), channel_id=1, source_target_pairs={{0,8},{8,0},{1,9},{9,1},{2,10},{10,2},{3,11},{11,3},{4,12},{12,4},... | collective-permute-start | bytes 3145736 | tf_op jit(solution)/shard_map/ppermute | solution.py:278
  11.5 2.5 %collective-permute-done.got = f32[4,128,512]{2,1,0:T(8,128)S(1)} collective-permute-done((f32[4,128,512]{2,1,0:T(8,128)}, f32[4,128,512]{2,1,0:T(8,128)S(1)}, u32[]{:S(2)}, u32[]{:S(2)}) %collective-permute-start) | collective-permute-done | bytes 1048608 | tf_op jit(solution)/shard_map/ppermute | solution.py:278
  14.0 1.0 copy-done.2
  15.0 2.7 %state.1 = (bf16[4,256,512]{2,1,0:T(8,128)(2,1)}, f32[4,128,128]{2,1,0:T(8,128)}, f32[512,128]{1,0:T(8,128)}) custom-call(s32[1]{0:T(128)} %bitcast.c, bf16[128,1024]{1,0:T(8,128)(2,1)} %q.3, bf16[128,1024]{1,0:T(8,128)(2,1)} %k.3, bf16[128,1024]{1,0:T(8,128)(2,1)} %v.3, bf16[128,1024]{1,0:T(8,128)(2,1)} %g.3, f32[4,128,512]{2,1,0:T(8,128)} %copy-done.2), custom_call_target="tpu_custom_call" | custom-call | tf_op jit(solution)/shard_map/state/pallas_call | solution.py:42
  17.7 19.2 %all_to_all.25 = f32[32,1,2048]{2,1,0:T(1,128)} all-to-all(f32[32,1,2048]{2,1,0:T(1,128)} %bitcast.19), channel_id=1, replica_groups=mesh['chip'=32,'core'=2,'head'=8] {'chip'}, dimensions={0} | all-to-all | bytes 524288 | tf_op jit(solution)/shard_map/all_to_all | solution.py:272
  36.9 1.7 %earlier.1 = f32[512,128]{1,0:T(8,128)} custom-call(s32[1]{0:T(128)} %bitcast.c, f32[512,128]{1,0:T(8,128)} %bitcast.17), custom_call_target="tpu_custom_call" | custom-call | tf_op jit(solution)/shard_map/earlier/pallas_call | solution.py:42
  38.6 4.6 %all-to-all-start.1 = ((f32[32,1,2048]{2,1,0:T(1,128)}), f32[32,1,2048]{2,1,0:T(1,128)S(1)}, u32[]{:S(2)}, u32[]{:S(2)}) async-start(f32[32,1,2048]{2,1,0:T(1,128)} %bitcast.16), calls=%async_computation.1 | async-start | bytes 524288 | tf_op jit(solution)/shard_map/all_to_all | solution.py:272
  43.2 3.4 %local.1 = (bf16[2,4,128,128]{3,2,1,0:T(8,128)(2,1)}, f32[256,512]{1,0:T(8,128)}) custom-call(s32[1]{0:T(128)} %bitcast.c, bf16[4,256,512]{2,1,0:T(8,128)(2,1)} %get-tuple-element.23.rows), custom_call_target="tpu_custom_call" | custom-call | tf_op jit(solution)/shard_map/local/pallas_call | solution.py:42
  46.6 7.2 %all-to-all-done.1 = f32[32,1,2048]{2,1,0:T(1,128)S(1)} async-done(((f32[32,1,2048]{2,1,0:T(1,128)}), f32[32,1,2048]{2,1,0:T(1,128)S(1)}, u32[]{:S(2)}, u32[]{:S(2)}) %all-to-all-start.1) | async-done | bytes 262176 | tf_op jit(solution)/shard_map/all_to_all | solution.py:272
  54.6 2.6 %attn.1 = (f32[256,512]{1,0:T(8,128)}, f32[16,4,128]{2,1,0:T(4,128)}) custom-call(s32[1]{0:T(128)} %bitcast.c, bf16[4,256,512]{2,1,0:T(8,128)(2,1)} %get-tuple-element.23.rows, f32[256,512]{1,0:T(8,128)} %get-tuple-element.25.intra, f32[4,128,128]{2,1,0:T(8,128)} %get-tuple-element.26.first, f32[512,128]{1,0:T(8,128)} %bitcast.11, f32[1,1024]{1,0:T(1,128)} %bitcast.20), custom_call_target="tpu_custom_call" | custom-call | tf_op jit(solution)/shard_map/attn/pallas_call | solution.py:42
  57.2 17.5 %all_to_all.26.parts = f32[16,4,128]{2,1,0:T(4,128)} all-to-all(f32[16,4,128]{2,1,0:T(4,128)} %get-tuple-element.29), channel_id=1, replica_groups=mesh['chip'=32,'core'=2,'head'=8] {'core','head'}, dimensions={0} | all-to-all | bytes 65536 | tf_op jit(solution)/shard_map/all_to_all | solution.py:299
  74.7 2.7 %grad.1 = (f32[256,512]{1,0:T(8,128)}, f32[4,128,128]{2,1,0:T(8,128)}, f32[544,128]{1,0:T(8,128)}) custom-call(s32[1]{0:T(128)} %bitcast.c, bf16[4,256,512]{2,1,0:T(8,128)(2,1)} %get-tuple-element.23.rows, f32[256,512]{1,0:T(8,128)} %get-tuple-element.28.flat, f32[1,1024]{1,0:T(1,128)} %bitcast.21, f32[16,4,128]{2,1,0:T(4,128)} %all_to_all.26.parts), custom_call_target="tpu_custom_call" | custom-call | tf_op jit(solution)/shard_map/grad/pallas_call | solution.py:42
  77.4 16.3 %all_to_all.27 = f32[32,1,2176]{2,1,0:T(1,128)} all-to-all(f32[32,1,2176]{2,1,0:T(1,128)} %bitcast.18), channel_id=1, replica_groups=mesh['chip'=32,'core'=2,'head'=8] {'chip'}, dimensions={0} | all-to-all | bytes 557056 | tf_op jit(solution)/shard_map/all_to_all | solution.py:272
  93.7 1.7 %later.1 = f32[544,128]{1,0:T(8,128)} custom-call(s32[1]{0:T(128)} %bitcast.c, f32[544,128]{1,0:T(8,128)} %bitcast.14), custom_call_target="tpu_custom_call" | custom-call | tf_op jit(solution)/shard_map/later/pallas_call | solution.py:42
  95.4 4.6 %all-to-all-start.4 = ((f32[32,1,2176]{2,1,0:T(1,128)}), f32[32,1,2176]{2,1,0:T(1,128)S(1)}, u32[]{:S(2)}, u32[]{:S(2)}) async-start(f32[32,1,2176]{2,1,0:T(1,128)} %bitcast.13), calls=%async_computation.4 | async-start | bytes 557056 | tf_op jit(solution)/shard_map/all_to_all | solution.py:272
  100.1 4.7 %query.1 = (f32[256,512]{1,0:T(8,128)}, f32[256,512]{1,0:T(8,128)}, f32[256,512]{1,0:T(8,128)}) custom-call(s32[1]{0:T(128)} %bitcast.c, bf16[4,256,512]{2,1,0:T(8,128)(2,1)} %get-tuple-element.23.rows, bf16[2,4,128,128]{3,2,1,0:T(8,128)(2,1)} %get-tuple-element.24.probs, f32[256,512]{1,0:T(8,128)} %get-tuple-element.30.gd, f32[512,128]{1,0:T(8,128)} %bitcast.12, ...), custom_call_target="tpu_custom_call" | custom-call | tf_op jit(solution)/shard_map/query/pallas_call | solution.py:42
  104.8 5.9 %all-to-all-done.4 = f32[32,1,2176]{2,1,0:T(1,128)S(1)} async-done(((f32[32,1,2176]{2,1,0:T(1,128)}), f32[32,1,2176]{2,1,0:T(1,128)S(1)}, u32[]{:S(2)}, u32[]{:S(2)}) %all-to-all-start.4) | async-done | bytes 278560 | tf_op jit(solution)/shard_map/all_to_all | solution.py:272
  110.7 0.7 copy-done.1
  111.4 4.1 %key.1 = (f32[3,128,512]{2,1,0:T(8,128)}, f32[392,512]{1,0:T(8,128)}) custom-call(s32[1]{0:T(128)} %bitcast.c, bf16[4,256,512]{2,1,0:T(8,128)(2,1)} %get-tuple-element.23.rows, f32[256,512]{1,0:T(8,128)} %get-tuple-element.31.gq, f32[256,512]{1,0:T(8,128)} %get-tuple-element.32.gk, f32[256,512]{1,0:T(8,128)} %get-tuple-element.33.gv, ...), custom_call_target="tpu_custom_call" | custom-call | tf_op jit(solution)/shard_map/key/pallas_call | solution.py:42
  115.5 5.8 %collective-permute-start.1 = (f32[392,512]{1,0:T(8,128)}, f32[392,512]{1,0:T(8,128)S(1)}, u32[]{:S(2)}, u32[]{:S(2)}) collective-permute-start(f32[392,512]{1,0:T(8,128)} %get-tuple-element.37.gain_keep), channel_id=1, source_target_pairs={{0,8},{8,0},{1,9},{9,1},{2,10},{10,2},{3,11},{11,3},{4,12},{12,4},... | collective-permute-start | bytes 2408456 | tf_op jit(solution)/shard_map/ppermute | solution.py:323
  121.3 2.1 %collective-permute-done.1.got = f32[392,512]{1,0:T(8,128)S(1)} collective-permute-done((f32[392,512]{1,0:T(8,128)}, f32[392,512]{1,0:T(8,128)S(1)}, u32[]{:S(2)}, u32[]{:S(2)}) %collective-permute-start.1) | collective-permute-done | bytes 802848 | tf_op jit(solution)/shard_map/ppermute | solution.py:323
  123.4 0.9 copy-done.3
  124.3 2.3 %final.1 = (bf16[128,1024]{1,0:T(8,128)(2,1)}, bf16[128,1024]{1,0:T(8,128)(2,1)}, bf16[128,1024]{1,0:T(8,128)(2,1)}, f32[1,1024]{1,0:T(1,128)}) custom-call(s32[1]{0:T(128)} %bitcast.c, f32[3,128,512]{2,1,0:T(8,128)} %get-tuple-element.36.keep, f32[392,512]{1,0:T(8,128)} %get-tuple-element.37.gain_keep, f32[392,512]{1,0:T(8,128)} %copy-done.3), custom_call_target="tpu_custom_call" | custom-call | tf_op jit(solution)/shard_map/final/pallas_call | solution.py:42
  (5 shorter events, 0.7 us)
Async XLA Ops:
  2.8 11.2 %collective-permute-start = (f32[4,128,512]{2,1,0:T(8,128)}, f32[4,128,512]{2,1,0:T(8,128)S(1)}, u32[]{:S(2)}, u32[]{:S(2)}) collective-permute-start(f32[4,128,512]{2,1,0:T(8,128)} %send.1), channel_id=1, source_target_pairs={{0,8},{8,0},{1,9},{9,1},{2,10},{10,2},{3,11},{11,3},{4,12},{12,4},... | collective-permute-start | bytes 3145736 | tf_op jit(solution)/shard_map/ppermute | solution.py:278
  14.0 1.0 copy-start.2
  38.6 15.2 %all-to-all-start.1 = ((f32[32,1,2048]{2,1,0:T(1,128)}), f32[32,1,2048]{2,1,0:T(1,128)S(1)}, u32[]{:S(2)}, u32[]{:S(2)}) async-start(f32[32,1,2048]{2,1,0:T(1,128)} %bitcast.16), calls=%async_computation.1 | async-start | bytes 524288 | tf_op jit(solution)/shard_map/all_to_all | solution.py:272
  53.9 0.7 copy-start
  95.4 15.2 %all-to-all-start.4 = ((f32[32,1,2176]{2,1,0:T(1,128)}), f32[32,1,2176]{2,1,0:T(1,128)S(1)}, u32[]{:S(2)}, u32[]{:S(2)}) async-start(f32[32,1,2176]{2,1,0:T(1,128)} %bitcast.13), calls=%async_computation.4 | async-start | bytes 557056 | tf_op jit(solution)/shard_map/all_to_all | solution.py:272
  110.7 0.7 copy-start.1
  115.5 7.9 %collective-permute-start.1 = (f32[392,512]{1,0:T(8,128)}, f32[392,512]{1,0:T(8,128)S(1)}, u32[]{:S(2)}, u32[]{:S(2)}) collective-permute-start(f32[392,512]{1,0:T(8,128)} %get-tuple-element.37.gain_keep), channel_id=1, source_target_pairs={{0,8},{8,0},{1,9},{9,1},{2,10},{10,2},{3,11},{11,3},{4,12},{12,4},... | collective-permute-start | bytes 2408456 | tf_op jit(solution)/shard_map/ppermute | solution.py:323
  123.4 0.9 copy-start.3

commit v2 on v1

v2 whole, which is shorter than its diff:
```python
import functools

import jax
import jax.numpy as jnp
from jax import lax
from jax.experimental import pallas as pl
from jax.experimental.pallas import tpu as pltpu
from jax.sharding import Mesh, PartitionSpec as P

DH = 128
EPS = 1e-06
F32 = jnp.float32
BF16 = jnp.bfloat16


def dot(a, b, ca, cb):
    return lax.dot_general(a, b, (((ca,), (cb,)), ((), ())), preferred_element_type=F32)


def split(x):
    hi = x.astype(BF16)
    return hi, (x - hi.astype(F32)).astype(BF16)


def dot2(a, hi, lo, cb):
    return dot(jnp.concatenate([a, a], 1), jnp.concatenate([hi, lo], cb), 1, cb)


def causal():
    rows = lax.broadcasted_iota(jnp.int32, (DH, DH), 0)
    cols = lax.broadcasted_iota(jnp.int32, (DH, DH), 1)
    return rows >= cols


def hs(h):
    return slice(h * DH, (h + 1) * DH)


def call(name, body, core, ins, outs, scratch=(), far=()):
    vmem = pl.BlockSpec(memory_space=pltpu.VMEM)
    count = len(ins)
    ins = [
        x if i in far else pltpu.with_memory_space_constraint(x, pltpu.VMEM)
        for i, x in enumerate(ins)
    ]
    outs = [
        o if count + i in far else pltpu.VMEM(o.shape, o.dtype) for i, o in enumerate(outs)
    ]
    return pl.pallas_call(
        body,
        name=name,
        out_shape=outs,
        in_specs=[pl.BlockSpec(memory_space=pltpu.SMEM)] + [vmem] * len(ins),
        out_specs=[vmem] * len(outs),
        scratch_shapes=list(scratch),
        compiler_params=pltpu.CompilerParams(vmem_limit_bytes=16 * 2**20),
    )(core, *ins)


def sds(shape, dtype):
    return jax.ShapeDtypeStruct(shape, dtype)


def half_of(ref, at, half):
    return ref[:, pl.ds(pl.multiple_of(at * half, DH), half)]


def send_body(c, q, k, v, g, out):
    for i, ref in enumerate((q, k, v, g)):
        out[i] = half_of(ref, 1 - c[0], out.shape[2]).astype(F32)


def place(c, ref, got, row, out, at):
    mine = pl.multiple_of(c[0] * DH, DH)
    other = pl.multiple_of((1 - c[0]) * DH, DH)
    out[at, pl.ds(mine, DH), :] = half_of(ref, c[0], out.shape[2])
    out[at, pl.ds(other, DH), :] = got[row].astype(BF16)


def state_body(c, k, v, got, kv, first, total):
    place(c, k, got, 1, kv, 0)
    place(c, v, got, 2, kv, 1)
    for h in range(first.shape[0]):
        s0 = dot(kv[0, 0:DH, hs(h)], kv[1, 0:DH, hs(h)], 0, 0)
        s1 = dot(kv[0, DH : 2 * DH, hs(h)], kv[1, DH : 2 * DH, hs(h)], 0, 0)
        first[h] = s0
        total[hs(h), :] = s0 + s1


def local_body(c, q, g, got, kv, qg, probs, intra):
    place(c, q, got, 0, qg, 0)
    place(c, g, got, 3, qg, 1)
    mask = causal()
    heads = probs.shape[1]
    for b in range(2):
        r = slice(b * DH, (b + 1) * DH)
        for h in range(heads):
            p = dot(qg[0, r, hs(h)], kv[0, r, hs(h)], 1, 1)
            p = jnp.where(mask, p, 0.0).astype(BF16)
            probs[b, h] = p
            intra[r, hs(h)] = dot(p, kv[1, r, hs(h)], 1, 0)


def earlier_body(n, c, x, out):
    share = x.shape[0] // n
    acc = jnp.zeros((share, DH), F32)
    for i in range(n):
        out[i * share : (i + 1) * share, :] = acc
        if i + 1 < n:
            acc = acc + x[i * share : (i + 1) * share, :]


def attn_body(c, qg, intra, first, prior, gain, flat, parts):
    heads = first.shape[0]
    my_gain = half_of(gain, c[0], heads * DH)
    for b in range(2):
        r = slice(b * DH, (b + 1) * DH)
        square = jnp.zeros((DH, DH), F32)
        cross = jnp.zeros((DH, DH), F32)
        for h in range(heads):
            p = prior[hs(h), :]
            if b == 1:
                p = p + first[h]
            hi, lo = split(p)
            f = intra[r, hs(h)] + dot2(qg[0, r, hs(h)], hi, lo, 0)
            flat[r, hs(h)] = f
            square = square + f * f
            cross = cross + (qg[1, r, hs(h)].astype(F32) * my_gain[:, hs(h)]) * f
        sq = jnp.sum(square.T, axis=0, keepdims=True)
        cr = jnp.sum(cross.T, axis=0, keepdims=True)
        for j in range(parts.shape[0]):
            parts[j, b : b + 1, :] = sq
            parts[j, 2 + b : 3 + b, :] = cr


def grad_body(n, width, c, qg, flat, gain, parts, gd, second, out):
    heads = second.shape[0]
    own = heads * DH // n
    my_gain = half_of(gain, c[0], heads * DH)
    total = jnp.sum(parts[...], axis=0)
    gain_rows = [jnp.zeros((1, DH), F32) for _ in range(heads)]
    sums = [None] * heads
    for b in range(2):
        r = slice(b * DH, (b + 1) * DH)
        inverse = lax.rsqrt(total[b : b + 1, :] / width + EPS)
        scale = inverse * total[2 + b : 3 + b, :] / width
        inverse = jnp.broadcast_to(inverse, (DH, DH)).T
        scale = jnp.broadcast_to(scale, (DH, DH)).T
        for h in range(heads):
            g = qg[1, r, hs(h)].astype(F32)
            normed = flat[r, hs(h)] * inverse
            d = inverse * (g * my_gain[:, hs(h)] - normed * scale)
            gd[r, hs(h)] = d
            gain_rows[h] = gain_rows[h] + jnp.sum(g * normed, axis=0, keepdims=True)
            hi, lo = split(d)
            q = qg[0, r, hs(h)]
            s = dot(q, lo, 0, 0) + dot(q, hi, 0, 0)
            if b == 1:
                second[h] = s
                sums[h] = sums[h] + s
            else:
                sums[h] = s
    for j in range(n):
        h, at = divmod(j * own, DH)
        out[j * (own + 1) : j * (own + 1) + own, :] = sums[h][at : at + own, :]
        out[j * (own + 1) + own : (j + 1) * (own + 1), :] = gain_rows[j % heads]


def query_body(c, qg, kv, probs, gd, prior, first, gq, gk, gv):
    mask = causal()
    heads = first.shape[0]
    for b in range(2):
        r = slice(b * DH, (b + 1) * DH)
        for h in range(heads):
            q, k, v = qg[0, r, hs(h)], kv[0, r, hs(h)], kv[1, r, hs(h)]
            hi, lo = split(gd[r, hs(h)])
            dp = dot(hi, v, 1, 1)
            dp = jnp.where(mask, dp, 0.0).astype(BF16)
            p = prior[hs(h), :]
            if b == 1:
                p = p + first[h]
            phi, plo = split(p)
            t = dot(lo, phi, 1, 1) + dot2(hi, phi, plo, 1)
            gq[r, hs(h)] = dot(dp, k, 1, 0) + t
            gk[r, hs(h)] = dot(dp, q, 0, 0)
            gv[r, hs(h)] = dot(probs[b, h], hi, 0, 0)


def later_body(n, c, x, out):
    share = x.shape[0] // n
    own = share - 1
    acc = jnp.zeros((own, DH), F32)
    gain = jnp.zeros((1, DH), F32)
    for i in range(n):
        gain = gain + x[i * share + own : (i + 1) * share, :]
    for i in reversed(range(n)):
        out[i * share : i * share + own, :] = acc
        out[i * share + own : (i + 1) * share, :] = gain
        if i:
            acc = acc + x[i * share : i * share + own, :]


def key_body(n, c, kv, gq, gk, gv, second, got, keep, send, later):
    heads = second.shape[0]
    own = heads * DH // n
    for j in range(n):
        later[j * own : (j + 1) * own, :] = got[j * (own + 1) : j * (own + 1) + own, :]
    mine = pl.multiple_of(c[0] * DH, DH)
    other = pl.multiple_of((1 - c[0]) * DH, DH)
    keep[0] = gq[pl.ds(mine, DH), :]
    send[0:DH, :] = gq[pl.ds(other, DH), :]
    for h in range(heads):
        send[3 * DH : 3 * DH + 8, hs(h)] = jnp.broadcast_to(
            got[h * (own + 1) + own : (h + 1) * (own + 1), :], (8, DH)
        )
        one = later[hs(h), :]
        zero_hi, zero_lo = split(one + second[h])
        one_hi, one_lo = split(one)

        def put(b, kept, sent, hi, lo):
            r = slice(b * DH, (b + 1) * DH)
            k, v = kv[0, r, hs(h)], kv[1, r, hs(h)]
            dk = gk[r, hs(h)] + dot2(v, hi, lo, 1)
            dv = gv[r, hs(h)] + dot2(k, hi, lo, 0)
            if kept is not None:
                kept[1, :, hs(h)] = dk
                kept[2, :, hs(h)] = dv
            else:
                sent[DH : 2 * DH, hs(h)] = dk
                sent[2 * DH : 3 * DH, hs(h)] = dv

        @pl.when(c[0] == 0)
        def _():
            put(0, keep, None, zero_hi, zero_lo)
            put(1, None, send, one_hi, one_lo)

        @pl.when(c[0] == 1)
        def _():
            put(0, None, send, zero_hi, zero_lo)
            put(1, keep, None, one_hi, one_lo)


def final_body(c, keep, sent, got, gq, gk, gv, gain):
    half = keep.shape[2]

    def put(at, away):
        for i, ref in enumerate((gq, gk, gv)):
            ref[:, at : at + half] = keep[i].astype(BF16)
            ref[:, away : away + half] = got[i * DH : (i + 1) * DH, :].astype(BF16)
        gain[:, at : at + half] = sent[3 * DH : 3 * DH + 1, :]
        gain[:, away : away + half] = got[3 * DH : 3 * DH + 1, :]

    @pl.when(c[0] == 0)
    def _():
        put(0, half)

    @pl.when(c[0] == 1)
    def _():
        put(half, 0)


def shards(query_rows, key_rows, value_rows, grad_output, norm_gain):
    count, width = query_rows.shape
    half = width // 2
    heads = half // DH
    both = 2 * count
    chips = lax.axis_size("chip")
    columns = lax.axis_size("head")
    full = columns * width
    at = lax.axis_index("core")
    core = at.astype(jnp.int32).reshape(1)
    swap = [(0, 1), (1, 0)]
    args = (query_rows, key_rows, value_rows, grad_output)
    gains = norm_gain.reshape(1, width)
    act = sds((both, half), F32)
    pair = sds((2, both, half), BF16)
    state = sds((heads, DH, DH), F32)
    flat_state = sds((heads * DH, DH), F32)
    padded = sds((heads * DH + chips, DH), F32)

    def exchange(x):
        y = lax.all_to_all(
            x.reshape(chips, 1, -1), "chip", split_axis=0, concat_axis=0, tiled=True
        )
        return y.reshape(x.shape)

    sent = call("send", send_body, core, args, [sds((4, count, half), F32)], far=(0, 3))[0]
    got = lax.ppermute(sent, "core", swap)
    kv, first, total = call(
        "state", state_body, core, (key_rows, value_rows, got), [pair, state, flat_state]
    )
    mine_states = exchange(total)
    qg, probs, intra = call(
        "local", local_body, core, (query_rows, grad_output, got, kv),
        [pair, sds((2, heads, DH, DH), BF16), act], far=(0, 1, 5),
    )
    sums = call(
        "earlier", functools.partial(earlier_body, chips), core, (mine_states,), [flat_state]
    )[0]
    prior = exchange(sums)
    flat, parts = call(
        "attn", attn_body, core, (qg, intra, first, prior, gains),
        [act, sds((2 * columns, 4, DH), F32)],
    )
    parts = lax.all_to_all(parts, ("core", "head"), split_axis=0, concat_axis=0, tiled=True)
    gd, second, block = call(
        "grad", functools.partial(grad_body, chips, full), core, (qg, flat, gains, parts),
        [act, state, padded],
    )
    mine_grads = exchange(block)
    gq, gk, gv = call(
        "query", query_body, core, (qg, kv, probs, gd, prior, first), [act, act, act],
        far=(2,),
    )
    later_sums = call(
        "later", functools.partial(later_body, chips), core, (mine_grads,), [padded]
    )[0]
    later = exchange(later_sums)
    keep, send = call(
        "key", functools.partial(key_body, chips), core, (kv, gq, gk, gv, second, later),
        [sds((3, count, half), F32), sds((3 * count + 8, half), F32)],
        scratch=[pltpu.VMEM(flat_state.shape, F32)],
    )
    back = lax.ppermute(send, "core", swap)
    gq, gk, gv, gain = call(
        "final", final_body, core, (keep, send, back),
        [sds((count, width), BF16)] * 3 + [sds((1, width), F32)], far=(3, 4, 5, 6),
    )
    return gq, gk, gv, gain.reshape(width)


def solution(mesh):
    names = dict(mesh.shape)
    inner = Mesh(
        mesh.devices.reshape(names["seq"] // 2, 2, names["head"]), ("chip", "core", "head")
    )
    seq = ("chip", "core")
    placed = (P(seq, "head"),) * 4 + (P("head"),)
    return jax.shard_map(
        shards,
        mesh=inner,
        in_specs=placed,
        out_specs=(P(seq, "head"),) * 3 + (P("head"),),
        check_vma=False,
    )
```

time: 127 us -> 115 us (0.906)
  Pallas kernels: 28.2 us -> 7.88 us
  local copies, waits for them, and re-layouts: 3.3 us -> 11 us
  waiting for transfers between devices: 17.7 us -> 19.7 us
  blocking collectives: 53.1 us -> 51.2 us
    pallas_call x10, Pallas kernels: 28.2 us -> 7.88 us  [call(): pl.pallas_call(body, name=name, out_shape=outs, in_specs=[pl.BlockSpec(me...]
    unnamed x8 -> x32, local copies, waits for them, and re-layouts: 3.3 us -> 11 us
    all_to_all x2, waiting for transfers between devices: 13.1 us -> 15.6 us  [exchange(): lax.all_to_all(x.reshape(chips, 1, -1), 'chip', split_axis=0, concat_axis...]
    all_to_all x2, blocking collectives: 35.5 us -> 34 us  [exchange(): lax.all_to_all(x.reshape(chips, 1, -1), 'chip', split_axis=0, concat_axis...]
  transfers between devices with their start and end apart: 4 -> 4, of which waited for: 4 -> 4; matrix products, arithmetic and copies ran while one was open for 0% -> 0% of each run, Pallas kernels for 6% -> 3%
where the time goes in v2:
time: 115 us
  blocking collectives  51.2 us (45%)
  starting transfers between devices  24 us (21%)
  waiting for transfers between devices  19.7 us (17%)
  local copies, waits for them, and re-layouts  11 us (10%)
  Pallas kernels  7.88 us (7%)
    all_to_all x2, blocking collectives, exchange(): lax.all_to_all(x.reshape(chips, 1, -1), 'chip', split_axis=0, concat_axis...  34 us
    all_to_all x1, blocking collectives, shards(): lax.all_to_all(parts, ('core', 'head'), split_axis=0, concat_axis=0, tile...  17.2 us
    all_to_all x2, waiting for transfers between devices, exchange(): lax.all_to_all(x.reshape(chips, 1, -1), 'chip', split_axis=0, concat_axis...  15.6 us
    unnamed x32, local copies, waits for them, and re-layouts  11 us
    all_to_all x2, starting transfers between devices, exchange(): lax.all_to_all(x.reshape(chips, 1, -1), 'chip', split_axis=0, concat_axis...  9.38 us
    ppermute x1, starting transfers between devices, shards(): got = lax.ppermute(sent, 'core', swap)  8.75 us
    pallas_call x10, Pallas kernels, call(): pl.pallas_call(body, name=name, out_shape=outs, in_specs=[pl.BlockSpec(me...  7.88 us
    ppermute x1, starting transfers between devices, shards(): back = lax.ppermute(send, 'core', swap)  5.83 us
  transfers between devices with their start and end apart: 4, of which 4 were waited for; matrix products, arithmetic and copies ran while one was open for 0% of the time, Pallas kernels for 3%

profile of v2, /device:TPU:1, one launch (start us, length us, event | category | flops | bytes accessed | tf_op | source)
XLA Modules:
  0.0 114.5 jit_solution(17220213956422183860)
XLA Ops:
  0.6 0.9 copy-done
  1.6 0.9 copy-done.2
  2.5 0.9 copy-done.4
  3.5 0.9 copy-done.6
  4.5 8.7 %collective-permute-start = (f32[4,128,512]{2,1,0:T(8,128)S(1)}, f32[4,128,512]{2,1,0:T(8,128)S(1)}, u32[]{:S(2)}, u32[]{:S(2)}) collective-permute-start(f32[4,128,512]{2,1,0:T(8,128)S(1)} %send.1), channel_id=1, source_target_pairs={{0,8},{8,0},{1,9},{9,1},{2,10},{10,2},{3,11},{11,3},{4,12},{12,4},... | collective-permute-start | bytes 3145736 | tf_op jit(solution)/shard_map/ppermute | solution.py:288
  13.3 2.3 %collective-permute-done.got = f32[4,128,512]{2,1,0:T(8,128)S(1)} collective-permute-done((f32[4,128,512]{2,1,0:T(8,128)S(1)}, f32[4,128,512]{2,1,0:T(8,128)S(1)}, u32[]{:S(2)}, u32[]{:S(2)}) %collective-permute-start) | collective-permute-done | bytes 1048608 | tf_op jit(solution)/shard_map/ppermute | solution.py:288
  15.8 18.9 %all_to_all.25 = f32[32,1,2048]{2,1,0:T(1,128)S(1)} all-to-all(f32[32,1,2048]{2,1,0:T(1,128)S(1)} %bitcast.17), channel_id=1, replica_groups=mesh['chip'=32,'core'=2,'head'=8] {'chip'}, dimensions={0} | all-to-all | bytes 524288 | tf_op jit(solution)/shard_map/all_to_all | solution.py:282
  35.5 4.7 %all-to-all-start.1 = ((f32[32,1,2048]{2,1,0:T(1,128)}), f32[32,1,2048]{2,1,0:T(1,128)S(1)}, u32[]{:S(2)}, u32[]{:S(2)}) async-start(f32[32,1,2048]{2,1,0:T(1,128)} %bitcast.3), calls=%async_computation.1 | async-start | bytes 524288 | tf_op jit(solution)/shard_map/all_to_all | solution.py:282
  40.3 1.4 %local.1 = (bf16[2,256,512]{2,1,0:T(8,128)(2,1)S(1)}, bf16[2,4,128,128]{3,2,1,0:T(8,128)(2,1)S(1)}, f32[256,512]{1,0:T(8,128)S(1)}) custom-call(s32[1]{0:T(128)} %bitcast.c, bf16[128,1024]{1,0:T(8,128)(2,1)S(1)} %copy-done.1, bf16[128,1024]{1,0:T(8,128)(2,1)S(1)} %copy-done.3, f32[4,128,512]{2,1,0:T(8,128)S(1)} %collective-permute-done.got, ...), custom_call_target="tpu_custom_call" | custom-call | tf_op jit(solution)/shard_map/local/pallas_call | solution.py:49
  42.5 8.4 %all-to-all-done.1 = f32[32,1,2048]{2,1,0:T(1,128)S(1)} async-done(((f32[32,1,2048]{2,1,0:T(1,128)}), f32[32,1,2048]{2,1,0:T(1,128)S(1)}, u32[]{:S(2)}, u32[]{:S(2)}) %all-to-all-start.1) | async-done | bytes 262176 | tf_op jit(solution)/shard_map/all_to_all | solution.py:282
  51.6 1.0 copy-done.8
  53.0 17.2 %all_to_all.26.parts = f32[16,4,128]{2,1,0:T(4,128)S(1)} all-to-all(f32[16,4,128]{2,1,0:T(4,128)S(1)} %get-tuple-element.31), channel_id=1, replica_groups=mesh['chip'=32,'core'=2,'head'=8] {'core','head'}, dimensions={0} | all-to-all | bytes 65536 | tf_op jit(solution)/shard_map/all_to_all | solution.py:305
  70.8 15.0 %all_to_all.27 = f32[32,1,2176]{2,1,0:T(1,128)S(1)} all-to-all(f32[32,1,2176]{2,1,0:T(1,128)S(1)} %bitcast.16), channel_id=1, replica_groups=mesh['chip'=32,'core'=2,'head'=8] {'chip'}, dimensions={0} | all-to-all | bytes 557056 | tf_op jit(solution)/shard_map/all_to_all | solution.py:282
  86.5 4.7 %all-to-all-start.4 = ((f32[32,1,2176]{2,1,0:T(1,128)}), f32[32,1,2176]{2,1,0:T(1,128)S(1)}, u32[]{:S(2)}, u32[]{:S(2)}) async-start(f32[32,1,2176]{2,1,0:T(1,128)} %bitcast.8), calls=%async_computation.4 | async-start | bytes 557056 | tf_op jit(solution)/shard_map/all_to_all | solution.py:282
  91.2 1.8 %query.1 = (f32[256,512]{1,0:T(8,128)S(1)}, f32[256,512]{1,0:T(8,128)S(1)}, f32[256,512]{1,0:T(8,128)S(1)}) custom-call(s32[1]{0:T(128)} %bitcast.c, bf16[2,256,512]{2,1,0:T(8,128)(2,1)S(1)} %get-tuple-element.25.qg, bf16[2,256,512]{2,1,0:T(8,128)(2,1)S(1)} %get-tuple-element.24.kv, bf16[2,4,128,128]{3,2,1,0:T(8,128)(2,1)S(1)} %get-tuple-element.26.probs, ...), custom_call_target="tpu_custom_call" | custom-call | tf_op jit(solution)/shard_map/query/pallas_call | solution.py:49
  93.8 0.8 copy-done.11
  94.7 7.1 %all-to-all-done.4 = f32[32,1,2176]{2,1,0:T(1,128)S(1)} async-done(((f32[32,1,2176]{2,1,0:T(1,128)}), f32[32,1,2176]{2,1,0:T(1,128)S(1)}, u32[]{:S(2)}, u32[]{:S(2)}) %all-to-all-start.4) | async-done | bytes 278560 | tf_op jit(solution)/shard_map/all_to_all | solution.py:282
  101.8 1.0 copy-done.10
  102.8 1.0 copy-done.12
  103.9 0.9 copy-done.14
  104.8 1.0 key.1
  105.8 5.8 %collective-permute-start.1 = (f32[392,512]{1,0:T(8,128)S(1)}, f32[392,512]{1,0:T(8,128)S(1)}, u32[]{:S(2)}, u32[]{:S(2)}) collective-permute-start(f32[392,512]{1,0:T(8,128)S(1)} %get-tuple-element.39.sent), channel_id=1, source_target_pairs={{0,8},{8,0},{1,9},{9,1},{2,10},{10,2},{3,11},{11,3},{4,12},{12,4},... | collective-permute-start | bytes 2408456 | tf_op jit(solution)/shard_map/ppermute | solution.py:324
  111.6 1.9 %collective-permute-done.1.got = f32[392,512]{1,0:T(8,128)S(1)} collective-permute-done((f32[392,512]{1,0:T(8,128)S(1)}, f32[392,512]{1,0:T(8,128)S(1)}, u32[]{:S(2)}, u32[]{:S(2)}) %collective-permute-start.1) | collective-permute-done | bytes 802848 | tf_op jit(solution)/shard_map/ppermute | solution.py:324
  113.6 1.0 final.1
  (29 shorter events, 5.1 us)
Async XLA Ops:
  0.6 1.0 copy-start
  1.6 0.9 copy-start.2
  2.5 0.9 copy-start.4
  3.5 0.9 copy-start.6
  4.4 11.1 %copy-start.5 = (bf16[128,1024]{1,0:T(8,128)(2,1)S(1)}, bf16[128,1024]{1,0:T(8,128)(2,1)}, u32[]{:S(2)}) copy-start(bf16[128,1024]{1,0:T(8,128)(2,1)} %k.3) | copy-start | bytes 786436
  4.5 11.0 %collective-permute-start = (f32[4,128,512]{2,1,0:T(8,128)S(1)}, f32[4,128,512]{2,1,0:T(8,128)S(1)}, u32[]{:S(2)}, u32[]{:S(2)}) collective-permute-start(f32[4,128,512]{2,1,0:T(8,128)S(1)} %send.1), channel_id=1, source_target_pairs={{0,8},{8,0},{1,9},{9,1},{2,10},{10,2},{3,11},{11,3},{4,12},{12,4},... | collective-permute-start | bytes 3145736 | tf_op jit(solution)/shard_map/ppermute | solution.py:288
  35.5 4.7 %copy-start.1 = (bf16[128,1024]{1,0:T(8,128)(2,1)S(1)}, bf16[128,1024]{1,0:T(8,128)(2,1)}, u32[]{:S(2)}) copy-start(bf16[128,1024]{1,0:T(8,128)(2,1)} %q.3) | copy-start | bytes 786436
  35.5 4.7 %copy-start.3 = (bf16[128,1024]{1,0:T(8,128)(2,1)S(1)}, bf16[128,1024]{1,0:T(8,128)(2,1)}, u32[]{:S(2)}) copy-start(bf16[128,1024]{1,0:T(8,128)(2,1)} %g.3) | copy-start | bytes 786436
  35.5 15.4 %all-to-all-start.1 = ((f32[32,1,2048]{2,1,0:T(1,128)}), f32[32,1,2048]{2,1,0:T(1,128)S(1)}, u32[]{:S(2)}, u32[]{:S(2)}) async-start(f32[32,1,2048]{2,1,0:T(1,128)} %bitcast.3), calls=%async_computation.1 | async-start | bytes 524288 | tf_op jit(solution)/shard_map/all_to_all | solution.py:282
  41.6 0.8 copy-start.7
  50.9 0.7 copy-start.15
  51.6 1.0 copy-start.8
  70.7 15.1 %copy-start.13 = (f32[4,128,128]{2,1,0:T(8,128)}, f32[4,128,128]{2,1,0:T(8,128)S(1)}, u32[]{:S(2)}) copy-start(f32[4,128,128]{2,1,0:T(8,128)S(1)} %get-tuple-element.36.second) | copy-start | bytes 786436
  86.5 15.2 %all-to-all-start.4 = ((f32[32,1,2176]{2,1,0:T(1,128)}), f32[32,1,2176]{2,1,0:T(1,128)S(1)}, u32[]{:S(2)}, u32[]{:S(2)}) async-start(f32[32,1,2176]{2,1,0:T(1,128)} %bitcast.8), calls=%async_computation.4 | async-start | bytes 557056 | tf_op jit(solution)/shard_map/all_to_all | solution.py:282
  93.0 0.8 copy-start.9
  93.8 0.8 copy-start.11
  101.8 1.0 copy-start.10
  102.8 1.0 copy-start.12
  103.9 0.9 copy-start.14
  105.8 7.8 %collective-permute-start.1 = (f32[392,512]{1,0:T(8,128)S(1)}, f32[392,512]{1,0:T(8,128)S(1)}, u32[]{:S(2)}, u32[]{:S(2)}) collective-permute-start(f32[392,512]{1,0:T(8,128)S(1)} %get-tuple-element.39.sent), channel_id=1, source_target_pairs={{0,8},{8,0},{1,9},{9,1},{2,10},{10,2},{3,11},{11,3},{4,12},{12,4},... | collective-permute-start | bytes 2408456 | tf_op jit(solution)/shard_map/ppermute | solution.py:324

commit v3 on v2

v3 whole, which is shorter than its diff:
```python
import functools

import jax
import jax.numpy as jnp
from jax import lax
from jax.experimental import pallas as pl
from jax.experimental.pallas import tpu as pltpu
from jax.sharding import Mesh, PartitionSpec as P

DH = 128
EPS = 1e-06
F32 = jnp.float32
BF16 = jnp.bfloat16


def dot(a, b, ca, cb):
    return lax.dot_general(a, b, (((ca,), (cb,)), ((), ())), preferred_element_type=F32)


def split(x):
    hi = x.astype(BF16)
    return hi, (x - hi.astype(F32)).astype(BF16)


def dot2(a, hi, lo, cb):
    return dot(jnp.concatenate([a, a], 1), jnp.concatenate([hi, lo], cb), 1, cb)


def causal():
    rows = lax.broadcasted_iota(jnp.int32, (DH, DH), 0)
    cols = lax.broadcasted_iota(jnp.int32, (DH, DH), 1)
    return rows >= cols


def hs(h):
    return slice(h * DH, (h + 1) * DH)


def call(name, body, core, ins, outs, scratch=(), far=()):
    vmem = pl.BlockSpec(memory_space=pltpu.VMEM)
    count = len(ins)
    ins = [
        x if i in far else pltpu.with_memory_space_constraint(x, pltpu.VMEM)
        for i, x in enumerate(ins)
    ]
    outs = [
        o if count + i in far else pltpu.VMEM(o.shape, o.dtype) for i, o in enumerate(outs)
    ]
    return pl.pallas_call(
        body,
        name=name,
        out_shape=outs,
        in_specs=[pl.BlockSpec(memory_space=pltpu.SMEM)] + [vmem] * len(ins),
        out_specs=[vmem] * len(outs),
        scratch_shapes=list(scratch),
        compiler_params=pltpu.CompilerParams(vmem_limit_bytes=16 * 2**20),
    )(core, *ins)


def sds(shape, dtype):
    return jax.ShapeDtypeStruct(shape, dtype)


def half_of(ref, at, half):
    return ref[:, pl.ds(pl.multiple_of(at * half, DH), half)]


def send_body(c, q, k, v, g, out):
    for i, ref in enumerate((q, k, v, g)):
        out[i] = ref[...].astype(F32)


def place(c, ref, got, row, out, at):
    mine = pl.multiple_of(c[0] * DH, DH)
    other = pl.multiple_of((1 - c[0]) * DH, DH)
    out[at, pl.ds(mine, DH), :] = half_of(ref, c[0], out.shape[2])
    out[at, pl.ds(other, DH), :] = got[row].astype(BF16)


def state_body(c, q, k, v, g, got, qg, kv, total):
    place(c, k, got, 1, kv, 0)
    place(c, v, got, 2, kv, 1)
    for h in range(total.shape[0] // DH):
        total[hs(h), :] = dot(kv[0, :, hs(h)], kv[1, :, hs(h)], 0, 0)
    place(c, q, got, 0, qg, 0)
    place(c, g, got, 3, qg, 1)


def first_state(kv, h):
    return dot(kv[0, 0:DH, hs(h)], kv[1, 0:DH, hs(h)], 0, 0)


def local_body(c, qg, kv, gain, intra, my_gain):
    my_gain[...] = half_of(gain, c[0], my_gain.shape[1])
    mask = causal()
    for h in range(intra.shape[1] // DH):
        hi, lo = split(first_state(kv, h))
        for b in range(2):
            r = slice(b * DH, (b + 1) * DH)
            q = qg[0, r, hs(h)]
            p = dot(q, kv[0, r, hs(h)], 1, 1)
            p = jnp.where(mask, p, 0.0).astype(BF16)
            t = dot(p, kv[1, r, hs(h)], 1, 0)
            if b == 1:
                t = t + dot2(q, hi, lo, 0)
            intra[r, hs(h)] = t


def earlier_body(n, c, x, out):
    share = x.shape[0] // n
    acc = jnp.zeros((share, DH), F32)
    for i in range(n):
        out[i * share : (i + 1) * share, :] = acc
        if i + 1 < n:
            acc = acc + x[i * share : (i + 1) * share, :]


def attn_body(c, qg, intra, prior, gain, flat, parts):
    square = [jnp.zeros((DH, DH), F32) for _ in range(2)]
    cross = [jnp.zeros((DH, DH), F32) for _ in range(2)]
    for h in range(intra.shape[1] // DH):
        hi, lo = split(prior[hs(h), :])
        for b in range(2):
            r = slice(b * DH, (b + 1) * DH)
            f = intra[r, hs(h)] + dot2(qg[0, r, hs(h)], hi, lo, 0)
            flat[r, hs(h)] = f
            square[b] = square[b] + f * f
            cross[b] = cross[b] + (qg[1, r, hs(h)].astype(F32) * gain[:, hs(h)]) * f
    for b in range(2):
        sq = jnp.sum(square[b].T, axis=0, keepdims=True)
        cr = jnp.sum(cross[b].T, axis=0, keepdims=True)
        for j in range(parts.shape[0]):
            parts[j, b : b + 1, :] = sq
            parts[j, 2 + b : 3 + b, :] = cr


def grad_body(n, width, c, qg, flat, gain, parts, gd, out):
    heads = gd.shape[1] // DH
    own = heads * DH // n
    total = jnp.sum(parts[...], axis=0)
    gain_rows = [jnp.zeros((1, DH), F32) for _ in range(heads)]
    sums = [None] * heads
    for b in range(2):
        r = slice(b * DH, (b + 1) * DH)
        inverse = lax.rsqrt(total[b : b + 1, :] / width + EPS)
        scale = inverse * total[2 + b : 3 + b, :] / width
        inverse = jnp.broadcast_to(inverse, (DH, DH)).T
        scale = jnp.broadcast_to(scale, (DH, DH)).T
        for h in range(heads):
            g = qg[1, r, hs(h)].astype(F32)
            normed = flat[r, hs(h)] * inverse
            d = inverse * (g * gain[:, hs(h)] - normed * scale)
            gd[r, hs(h)] = d
            gain_rows[h] = gain_rows[h] + jnp.sum(g * normed, axis=0, keepdims=True)
            hi, lo = split(d)
            q = qg[0, r, hs(h)]
            s = dot(q, lo, 0, 0) + dot(q, hi, 0, 0)
            sums[h] = s if b == 0 else sums[h] + s
    for j in range(n):
        h, at = divmod(j * own, DH)
        out[j * (own + 1) : j * (own + 1) + own, :] = sums[h][at : at + own, :]
        out[j * (own + 1) + own : (j + 1) * (own + 1), :] = gain_rows[j % heads]


def query_body(c, qg, kv, gd, prior, keepq, keep, send, all3):
    mask = causal()
    for h in range(gd.shape[1] // DH):
        first = first_state(kv, h)
        second = None
        for b in (1, 0):
            r = slice(b * DH, (b + 1) * DH)
            q, k, v = qg[0, r, hs(h)], kv[0, r, hs(h)], kv[1, r, hs(h)]
            hi, lo = split(gd[r, hs(h)])
            p = dot(q, k, 1, 1)
            p = jnp.where(mask, p, 0.0).astype(BF16)
            dp = dot(hi, v, 1, 1)
            dp = jnp.where(mask, dp, 0.0).astype(BF16)
            prior_b = prior[hs(h), :]
            if b == 1:
                prior_b = prior_b + first
            phi, plo = split(prior_b)
            t = dot(lo, phi, 1, 1) + dot2(hi, phi, plo, 1)
            all3[0, r, hs(h)] = dot(dp, k, 1, 0) + t
            dk = dot(dp, q, 0, 0)
            dv = dot(p, hi, 0, 0)
            if b == 1:
                second = split(dot(q, lo, 0, 0) + dot(q, hi, 0, 0))
            else:
                dk = dk + dot2(v, *second, 1)
                dv = dv + dot2(k, *second, 0)
            all3[1, r, hs(h)] = dk
            all3[2, r, hs(h)] = dv
    mine = pl.multiple_of(c[0] * DH, DH)
    other = pl.multiple_of((1 - c[0]) * DH, DH)
    keepq[...] = all3[0, pl.ds(mine, DH), :].astype(BF16)
    keep[...] = all3[1:3, pl.ds(mine, DH), :]
    send[...] = all3[:, pl.ds(other, DH), :]


def later_body(n, c, x, out):
    share = x.shape[0] // n
    own = share - 1
    acc = jnp.zeros((own, DH), F32)
    gain = jnp.zeros((1, DH), F32)
    for i in range(n):
        gain = gain + x[i * share + own : (i + 1) * share, :]
    for i in reversed(range(n)):
        out[i * share : i * share + own, :] = acc
        out[i * share + own : (i + 1) * share, :] = gain
        if i:
            acc = acc + x[i * share : i * share + own, :]


def final_body(n, c, k, v, keepq, keep, early, mine, other, gq, gk, gv, gain):
    half = keep.shape[2]
    own = half // n
    per = DH // own

    def put(at, away):
        gq[:, at : at + half] = keepq[...]
        gq[:, away : away + half] = early[0].astype(BF16)
        for base, sums, part, i in ((at, mine, keep, 0), (away, other, early, 1)):
            for h in range(half // DH):
                to = slice(base + h * DH, base + (h + 1) * DH)
                later = [
                    sums[j * (own + 1) : j * (own + 1) + own, :]
                    for j in range(h * per, (h + 1) * per)
                ]
                hi, lo = split(jnp.concatenate(later, 0))
                dk = part[i, :, hs(h)] + dot2(v[:, to], hi, lo, 1)
                dv = part[i + 1, :, hs(h)] + dot2(k[:, to], hi, lo, 0)
                gk[:, to] = dk.astype(BF16)
                gv[:, to] = dv.astype(BF16)
                gain[:, to] = sums[h * (own + 1) + own : (h + 1) * (own + 1), :]

    @pl.when(c[0] == 0)
    def _():
        put(0, half)

    @pl.when(c[0] == 1)
    def _():
        put(half, 0)


def shards(query_rows, key_rows, value_rows, grad_output, norm_gain):
    count, width = query_rows.shape
    half = width // 2
    heads = half // DH
    both = 2 * count
    chips = lax.axis_size("chip")
    columns = lax.axis_size("head")
    full = columns * width
    at = lax.axis_index("core")
    core = at.astype(jnp.int32).reshape(1)
    swap = [(0, 1), (1, 0)]
    args = (query_rows, key_rows, value_rows, grad_output)
    gains = norm_gain.reshape(1, width)
    act = sds((both, half), F32)
    pair = sds((2, both, half), BF16)
    flat_state = sds((heads * DH, DH), F32)
    padded = sds((heads * DH + chips, DH), F32)

    def exchange(x):
        y = lax.all_to_all(
            x.reshape(chips, 1, -1), "chip", split_axis=0, concat_axis=0, tiled=True
        )
        return y.reshape(x.shape)

    sent = pl.pallas_call(
        send_body,
        name="send",
        out_shape=pltpu.VMEM((4, count, half), F32),
        grid_spec=pltpu.PrefetchScalarGridSpec(
            num_scalar_prefetch=1,
            grid=(1,),
            in_specs=[pl.BlockSpec((count, half), lambda i, c: (0, 1 - c[0]))] * 4,
            out_specs=pl.BlockSpec(memory_space=pltpu.VMEM),
        ),
    )(core, *args)
    got = lax.ppermute(sent, "core", swap)
    qg, kv, total = call("state", state_body, core, (*args, got), [pair, pair, flat_state])
    mine_states = exchange(total)
    intra, my_gain = call(
        "local", local_body, core, (qg, kv, gains), [act, sds((1, half), F32)]
    )
    sums = call(
        "earlier", functools.partial(earlier_body, chips), core, (mine_states,), [flat_state]
    )[0]
    prior = exchange(sums)
    flat, parts = call(
        "attn", attn_body, core, (qg, intra, prior, my_gain),
        [act, sds((2 * columns, 4, DH), F32)],
    )
    parts = lax.all_to_all(parts, ("core", "head"), split_axis=0, concat_axis=0, tiled=True)
    gd, block = call(
        "grad", functools.partial(grad_body, chips, full), core, (qg, flat, my_gain, parts),
        [act, padded],
    )
    mine_grads = exchange(block)
    keepq, keep, send = call(
        "query", query_body, core, (qg, kv, gd, prior),
        [sds((count, half), BF16), sds((2, count, half), F32), sds((3, count, half), F32)],
        scratch=[pltpu.VMEM((3, both, half), F32)],
    )
    early = lax.ppermute(send, "core", swap)
    later_sums = call(
        "later", functools.partial(later_body, chips), core, (mine_grads,), [padded]
    )[0]
    later = exchange(later_sums)
    others = lax.ppermute(later, "core", swap)
    gq, gk, gv, gain = call(
        "final", functools.partial(final_body, chips), core,
        (key_rows, value_rows, keepq, keep, early, later, others),
        [sds((count, width), BF16)] * 3 + [sds((1, width), F32)], far=(7, 8, 9, 10),
    )
    return gq, gk, gv, gain.reshape(width)


def solution(mesh):
    names = dict(mesh.shape)
    inner = Mesh(
        mesh.devices.reshape(names["seq"] // 2, 2, names["head"]), ("chip", "core", "head")
    )
    seq = ("chip", "core")
    placed = (P(seq, "head"),) * 4 + (P("head"),)
    return jax.shard_map(
        shards,
        mesh=inner,
        in_specs=placed,
        out_specs=(P(seq, "head"),) * 3 + (P("head"),),
        check_vma=False,
    )
```

time: 115 us -> 106 us (0.922)
  local copies, waits for them, and re-layouts: 11 us -> 0.7 us
  waiting for transfers between devices: 19.7 us -> 15.6 us
  starting transfers between devices: 24 us -> 27.5 us
  Pallas kernels: 7.88 us -> 10.1 us
    unnamed x32 -> x10, local copies, waits for them, and re-layouts: 11 us -> 0.7 us
    ppermute x1 -> x2, starting transfers between devices: 5.83 us -> 9.47 us  [the longest x1 5.82 us: shards(): others = lax.ppermute(later, 'core', swap)]
    all_to_all x2, waiting for transfers between devices: 15.6 us -> 12.2 us  [exchange(): lax.all_to_all(x.reshape(chips, 1, -1), 'chip', split_axis=0, concat_axis...]
    pallas_call x0 -> x1, Pallas kernels: none -> 1.25 us  [shards(): pl.pallas_call(send_body, name='send', out_shape=pltpu.VMEM((4, count, ha...]
    pallas_call x10 -> x8, Pallas kernels: 7.88 us -> 8.81 us  [call(): pl.pallas_call(body, name=name, out_shape=outs, in_specs=[pl.BlockSpec(me...]
  transfers between devices with their start and end apart: 4 -> 5, of which waited for: 4 -> 4; matrix products, arithmetic and copies ran while one was open for 0% -> 0% of each run, Pallas kernels for 3% -> 4%
where the time goes in v3:
time: 106 us
  blocking collectives  51.2 us (48%)
  starting transfers between devices  27.5 us (26%)
  waiting for transfers between devices  15.6 us (15%)
  Pallas kernels  10.1 us (10%)
    all_to_all x2, blocking collectives, exchange(): lax.all_to_all(x.reshape(chips, 1, -1), 'chip', split_axis=0, concat_axis...  33.9 us
    all_to_all x1, blocking collectives, shards(): lax.all_to_all(parts, ('core', 'head'), split_axis=0, concat_axis=0, tile...  17.2 us
    all_to_all x2, waiting for transfers between devices, exchange(): lax.all_to_all(x.reshape(chips, 1, -1), 'chip', split_axis=0, concat_axis...  12.2 us
    all_to_all x2, starting transfers between devices, exchange(): lax.all_to_all(x.reshape(chips, 1, -1), 'chip', split_axis=0, concat_axis...  9.27 us
    pallas_call x8, Pallas kernels, call(): pl.pallas_call(body, name=name, out_shape=outs, in_specs=[pl.BlockSpec(me...  8.81 us
    ppermute x1, starting transfers between devices, shards(): got = lax.ppermute(sent, 'core', swap)  8.75 us
    ppermute x1, starting transfers between devices, shards(): others = lax.ppermute(later, 'core', swap)  5.82 us
    ppermute x1, starting transfers between devices, shards(): early = lax.ppermute(send, 'core', swap)  3.65 us
  transfers between devices with their start and end apart: 5, of which 4 were waited for; matrix products, arithmetic and copies ran while one was open for 0% of the time, Pallas kernels for 4%

profile of v3, /device:TPU:1, one launch (start us, length us, event | category | flops | bytes accessed | tf_op | source)
XLA Modules:
  0.0 105.7 jit_solution(16396064310806470799)
XLA Ops:
  0.7 1.2 %send.1 = f32[4,128,512]{2,1,0:T(8,128)S(1)} custom-call(s32[1]{0:T(128)} %bitcast.c, bf16[128,1024]{1,0:T(8,128)(2,1)} %q.3, bf16[128,1024]{1,0:T(8,128)(2,1)} %k.5, bf16[128,1024]{1,0:T(8,128)(2,1)} %v.5, bf16[128,1024]{1,0:T(8,128)(2,1)} %g.3), custom_call_target="tpu_custom_call" | custom-call | tf_op jit(solution)/shard_map/send/pallas_call | solution.py:269
  1.9 8.7 %collective-permute-start = (f32[4,128,512]{2,1,0:T(8,128)S(1)}, f32[4,128,512]{2,1,0:T(8,128)S(1)}, u32[]{:S(2)}, u32[]{:S(2)}) collective-permute-start(f32[4,128,512]{2,1,0:T(8,128)S(1)} %send.1), channel_id=1, source_target_pairs={{0,8},{8,0},{1,9},{9,1},{2,10},{10,2},{3,11},{11,3},{4,12},{12,4},... | collective-permute-start | bytes 3145736 | tf_op jit(solution)/shard_map/ppermute | solution.py:280
  10.7 2.3 %collective-permute-done.got = f32[4,128,512]{2,1,0:T(8,128)S(1)} collective-permute-done((f32[4,128,512]{2,1,0:T(8,128)S(1)}, f32[4,128,512]{2,1,0:T(8,128)S(1)}, u32[]{:S(2)}, u32[]{:S(2)}) %collective-permute-start) | collective-permute-done | bytes 1048608 | tf_op jit(solution)/shard_map/ppermute | solution.py:280
  13.0 0.4 state.1
  13.3 18.9 %all_to_all.25 = f32[32,1,2048]{2,1,0:T(1,128)S(1)} all-to-all(f32[32,1,2048]{2,1,0:T(1,128)S(1)} %bitcast.18), channel_id=1, replica_groups=mesh['chip'=32,'core'=2,'head'=8] {'chip'}, dimensions={0} | all-to-all | bytes 524288 | tf_op jit(solution)/shard_map/all_to_all | solution.py:264
  32.3 0.7 earlier.1
  33.0 4.6 %all-to-all-start.1 = ((f32[32,1,2048]{2,1,0:T(1,128)}), f32[32,1,2048]{2,1,0:T(1,128)S(1)}, u32[]{:S(2)}, u32[]{:S(2)}) async-start(f32[32,1,2048]{2,1,0:T(1,128)} %bitcast.4), calls=%async_computation.1 | async-start | bytes 524288 | tf_op jit(solution)/shard_map/all_to_all | solution.py:264
  37.6 0.0 copy-start.4
  37.6 0.7 copy-done.4
  38.3 1.4 %local.1 = (f32[256,512]{1,0:T(8,128)S(1)}, f32[1,512]{1,0:T(1,128)S(1)}) custom-call(s32[1]{0:T(128)} %bitcast.c, bf16[2,256,512]{2,1,0:T(8,128)(2,1)S(1)} %get-tuple-element.20.qg, bf16[2,256,512]{2,1,0:T(8,128)(2,1)S(1)} %get-tuple-element.21.kv, f32[1,1024]{1,0:T(1,128)S(1)} %bitcast.19), custom_call_target="tpu_custom_call" | custom-call | tf_op jit(solution)/shard_map/local/pallas_call | solution.py:49
  39.7 8.6 %all-to-all-done.1 = f32[32,1,2048]{2,1,0:T(1,128)S(1)} async-done(((f32[32,1,2048]{2,1,0:T(1,128)}), f32[32,1,2048]{2,1,0:T(1,128)S(1)}, u32[]{:S(2)}, u32[]{:S(2)}) %all-to-all-start.1) | async-done | bytes 262176 | tf_op jit(solution)/shard_map/all_to_all | solution.py:264
  48.2 0.4 attn.1
  48.7 17.2 %all_to_all.26.parts = f32[16,4,128]{2,1,0:T(4,128)S(1)} all-to-all(f32[16,4,128]{2,1,0:T(4,128)S(1)} %get-tuple-element.26), channel_id=1, replica_groups=mesh['chip'=32,'core'=2,'head'=8] {'core','head'}, dimensions={0} | all-to-all | bytes 65536 | tf_op jit(solution)/shard_map/all_to_all | solution.py:294
  65.9 0.5 grad.1
  66.4 15.0 %all_to_all.27 = f32[32,1,2176]{2,1,0:T(1,128)S(1)} all-to-all(f32[32,1,2176]{2,1,0:T(1,128)S(1)} %bitcast.17), channel_id=1, replica_groups=mesh['chip'=32,'core'=2,'head'=8] {'chip'}, dimensions={0} | all-to-all | bytes 557056 | tf_op jit(solution)/shard_map/all_to_all | solution.py:264
  81.4 0.8 later.1
  82.2 4.7 %all-to-all-start.4 = ((f32[32,1,2176]{2,1,0:T(1,128)}), f32[32,1,2176]{2,1,0:T(1,128)S(1)}, u32[]{:S(2)}, u32[]{:S(2)}) async-start(f32[32,1,2176]{2,1,0:T(1,128)} %bitcast.8), calls=%async_computation.4 | async-start | bytes 557056 | tf_op jit(solution)/shard_map/all_to_all | solution.py:264
  86.9 3.3 %query.1 = (bf16[128,512]{1,0:T(8,128)(2,1)S(1)}, f32[2,128,512]{2,1,0:T(8,128)S(1)}, f32[3,128,512]{2,1,0:T(8,128)}) custom-call(s32[1]{0:T(128)} %bitcast.c, bf16[2,256,512]{2,1,0:T(8,128)(2,1)S(1)} %get-tuple-element.20.qg, bf16[2,256,512]{2,1,0:T(8,128)(2,1)S(1)} %get-tuple-element.21.kv, f32[256,512]{1,0:T(8,128)S(1)} %get-tuple-element.27.gd, ...), custom_call_target="tpu_custom_call" | custom-call | tf_op jit(solution)/shard_map/query/pallas_call | solution.py:49
  90.2 3.6 %collective-permute-start.1 = (f32[3,128,512]{2,1,0:T(8,128)}, f32[3,128,512]{2,1,0:T(8,128)S(1)}, u32[]{:S(2)}, u32[]{:S(2)}) collective-permute-start(f32[3,128,512]{2,1,0:T(8,128)} %get-tuple-element.30), channel_id=1, source_target_pairs={{0,8},{8,0},{1,9},{9,1},{2,10},{10,2},{3,11},{11,3},{4,12},{12,4},... | collective-permute-start | bytes 2359304 | tf_op jit(solution)/shard_map/ppermute | solution.py:305
  93.8 3.6 %all-to-all-done.4 = f32[32,1,2176]{2,1,0:T(1,128)S(1)} async-done(((f32[32,1,2176]{2,1,0:T(1,128)}), f32[32,1,2176]{2,1,0:T(1,128)S(1)}, u32[]{:S(2)}, u32[]{:S(2)}) %all-to-all-start.4) | async-done | bytes 278560 | tf_op jit(solution)/shard_map/all_to_all | solution.py:264
  97.4 5.8 %collective-permute-start.2 = (f32[544,128]{1,0:T(8,128)S(1)}, f32[544,128]{1,0:T(8,128)S(1)}, u32[]{:S(2)}, u32[]{:S(2)}) collective-permute-start(f32[544,128]{1,0:T(8,128)S(1)} %bitcast.14), channel_id=1, source_target_pairs={{0,8},{8,0},{1,9},{9,1},{2,10},{10,2},{3,11},{11,3},{4,12},{12,4},... | collective-permute-start | bytes 835592 | tf_op jit(solution)/shard_map/ppermute | solution.py:310
  103.2 0.0 collective-permute-done.1.early
  103.3 1.2 %collective-permute-done.2.other = f32[544,128]{1,0:T(8,128)S(1)} collective-permute-done((f32[544,128]{1,0:T(8,128)S(1)}, f32[544,128]{1,0:T(8,128)S(1)}, u32[]{:S(2)}, u32[]{:S(2)}) %collective-permute-start.2) | collective-permute-done | bytes 278560 | tf_op jit(solution)/shard_map/ppermute | solution.py:310
  104.4 1.3 %final.1 = (bf16[128,1024]{1,0:T(8,128)(2,1)}, bf16[128,1024]{1,0:T(8,128)(2,1)}, bf16[128,1024]{1,0:T(8,128)(2,1)}, f32[1,1024]{1,0:T(1,128)}) custom-call(s32[1]{0:T(128)} %bitcast.c, bf16[128,1024]{1,0:T(8,128)(2,1)S(1)} %copy-done, bf16[128,1024]{1,0:T(8,128)(2,1)S(1)} %copy-done.1, bf16[128,512]{1,0:T(8,128)(2,1)S(1)} %get-tuple-element.28.keepq, ...), custom_call_target="tpu_custom_call" | custom-call | tf_op jit(solution)/shard_map/final/pallas_call | solution.py:49
  (8 shorter events, 0.0 us)
Async XLA Ops:
  0.6 12.3 %copy-start = (bf16[128,1024]{1,0:T(8,128)(2,1)S(1)}, bf16[128,1024]{1,0:T(8,128)(2,1)}, u32[]{:S(2)}) copy-start(bf16[128,1024]{1,0:T(8,128)(2,1)} %k.5) | copy-start | bytes 786436
  0.6 12.3 %copy-start.1 = (bf16[128,1024]{1,0:T(8,128)(2,1)S(1)}, bf16[128,1024]{1,0:T(8,128)(2,1)}, u32[]{:S(2)}) copy-start(bf16[128,1024]{1,0:T(8,128)(2,1)} %v.5) | copy-start | bytes 786436
  0.7 12.3 %copy-start.2 = (bf16[128,1024]{1,0:T(8,128)(2,1)S(1)}, bf16[128,1024]{1,0:T(8,128)(2,1)}, u32[]{:S(2)}) copy-start(bf16[128,1024]{1,0:T(8,128)(2,1)} %q.3) | copy-start | bytes 786436
  0.7 12.3 %copy-start.3 = (bf16[128,1024]{1,0:T(8,128)(2,1)S(1)}, bf16[128,1024]{1,0:T(8,128)(2,1)}, u32[]{:S(2)}) copy-start(bf16[128,1024]{1,0:T(8,128)(2,1)} %g.3) | copy-start | bytes 786436
  1.9 11.0 %collective-permute-start = (f32[4,128,512]{2,1,0:T(8,128)S(1)}, f32[4,128,512]{2,1,0:T(8,128)S(1)}, u32[]{:S(2)}, u32[]{:S(2)}) collective-permute-start(f32[4,128,512]{2,1,0:T(8,128)S(1)} %send.1), channel_id=1, source_target_pairs={{0,8},{8,0},{1,9},{9,1},{2,10},{10,2},{3,11},{11,3},{4,12},{12,4},... | collective-permute-start | bytes 3145736 | tf_op jit(solution)/shard_map/ppermute | solution.py:280
  33.0 15.2 %all-to-all-start.1 = ((f32[32,1,2048]{2,1,0:T(1,128)}), f32[32,1,2048]{2,1,0:T(1,128)S(1)}, u32[]{:S(2)}, u32[]{:S(2)}) async-start(f32[32,1,2048]{2,1,0:T(1,128)} %bitcast.4), calls=%async_computation.1 | async-start | bytes 524288 | tf_op jit(solution)/shard_map/all_to_all | solution.py:264
  37.6 0.7 copy-start.4
  82.2 15.2 %all-to-all-start.4 = ((f32[32,1,2176]{2,1,0:T(1,128)}), f32[32,1,2176]{2,1,0:T(1,128)S(1)}, u32[]{:S(2)}, u32[]{:S(2)}) async-start(f32[32,1,2176]{2,1,0:T(1,128)} %bitcast.8), calls=%async_computation.4 | async-start | bytes 557056 | tf_op jit(solution)/shard_map/all_to_all | solution.py:264
  90.2 13.1 %collective-permute-start.1 = (f32[3,128,512]{2,1,0:T(8,128)}, f32[3,128,512]{2,1,0:T(8,128)S(1)}, u32[]{:S(2)}, u32[]{:S(2)}) collective-permute-start(f32[3,128,512]{2,1,0:T(8,128)} %get-tuple-element.30), channel_id=1, source_target_pairs={{0,8},{8,0},{1,9},{9,1},{2,10},{10,2},{3,11},{11,3},{4,12},{12,4},... | collective-permute-start | bytes 2359304 | tf_op jit(solution)/shard_map/ppermute | solution.py:305
  97.4 7.0 %collective-permute-start.2 = (f32[544,128]{1,0:T(8,128)S(1)}, f32[544,128]{1,0:T(8,128)S(1)}, u32[]{:S(2)}, u32[]{:S(2)}) collective-permute-start(f32[544,128]{1,0:T(8,128)S(1)} %bitcast.14), channel_id=1, source_target_pairs={{0,8},{8,0},{1,9},{9,1},{2,10},{10,2},{3,11},{11,3},{4,12},{12,4},... | collective-permute-start | bytes 835592 | tf_op jit(solution)/shard_map/ppermute | solution.py:310

commit v4 on v3

--- a/solution.py
+++ b/solution.py
@@ -7,6 +7,7 @@
 from jax.experimental.pallas import tpu as pltpu
 from jax.sharding import Mesh, PartitionSpec as P
 
+
 DH = 128
 EPS = 1e-06
 F32 = jnp.float32
@@ -36,7 +37,7 @@
     return slice(h * DH, (h + 1) * DH)
 
 
-def call(name, body, core, ins, outs, scratch=(), far=()):
+def call(body, core, ins, outs, scratch=(), far=()):
     vmem = pl.BlockSpec(memory_space=pltpu.VMEM)
     count = len(ins)
     ins = [
@@ -48,7 +49,6 @@
     ]
     return pl.pallas_call(
         body,
-        name=name,
         out_shape=outs,
         in_specs=[pl.BlockSpec(memory_space=pltpu.SMEM)] + [vmem] * len(ins),
         out_specs=[vmem] * len(outs),
@@ -57,6 +57,19 @@
     )(core, *ins)
 
 
+def windowed(body, core, ins, in_specs, outs):
+    return pl.pallas_call(
+        body,
+        out_shape=[pltpu.VMEM(o.shape, o.dtype) for o in outs],
+        grid_spec=pltpu.PrefetchScalarGridSpec(
+            num_scalar_prefetch=1,
+            grid=(1,),
+            in_specs=in_specs,
+            out_specs=[pl.BlockSpec(memory_space=pltpu.VMEM)] * len(outs),
+        ),
+    )(core, *ins)
+
+
 def sds(shape, dtype):
     return jax.ShapeDtypeStruct(shape, dtype)
 
@@ -70,20 +83,20 @@
         out[i] = ref[...].astype(F32)
 
 
-def place(c, ref, got, row, out, at):
+def state_body(c, k, v, mine, send):
+    heads = mine.shape[0] // DH
+    for out, at in ((mine, c[0]), (send, 1 - c[0])):
+        for h in range(heads):
+            to = pl.ds(pl.multiple_of((at * heads + h) * DH, DH), DH)
+            out[hs(h), :] = dot(k[:, to], v[:, to], 0, 0)
+
+
+def place_body(c, q, k, v, g, got, qg, kv):
     mine = pl.multiple_of(c[0] * DH, DH)
     other = pl.multiple_of((1 - c[0]) * DH, DH)
-    out[at, pl.ds(mine, DH), :] = half_of(ref, c[0], out.shape[2])
-    out[at, pl.ds(other, DH), :] = got[row].astype(BF16)
-
-
-def state_body(c, q, k, v, g, got, qg, kv, total):
-    place(c, k, got, 1, kv, 0)
-    place(c, v, got, 2, kv, 1)
-    for h in range(total.shape[0] // DH):
-        total[hs(h), :] = dot(kv[0, :, hs(h)], kv[1, :, hs(h)], 0, 0)
-    place(c, q, got, 0, qg, 0)
-    place(c, g, got, 3, qg, 1)
+    for i, (ref, out, at) in enumerate(((q, qg, 0), (k, kv, 0), (v, kv, 1), (g, qg, 1))):
+        out[at, pl.ds(mine, DH), :] = ref[...]
+        out[at, pl.ds(other, DH), :] = got[i].astype(BF16)
 
 
 def first_state(kv, h):
@@ -106,7 +119,7 @@
             intra[r, hs(h)] = t
 
 
-def earlier_body(n, c, x, out):
+def earlier_body(n, c, x, after, out):
     share = x.shape[0] // n
     acc = jnp.zeros((share, DH), F32)
     for i in range(n):
@@ -266,50 +279,43 @@
         )
         return y.reshape(x.shape)
 
-    sent = pl.pallas_call(
-        send_body,
-        name="send",
-        out_shape=pltpu.VMEM((4, count, half), F32),
-        grid_spec=pltpu.PrefetchScalarGridSpec(
-            num_scalar_prefetch=1,
-            grid=(1,),
-            in_specs=[pl.BlockSpec((count, half), lambda i, c: (0, 1 - c[0]))] * 4,
-            out_specs=pl.BlockSpec(memory_space=pltpu.VMEM),
-        ),
-    )(core, *args)
+    all_cols = pl.BlockSpec((count, width), lambda i, c: (0, 0))
+    my_cols = pl.BlockSpec((count, half), lambda i, c: (0, c[0]))
+    away_cols = pl.BlockSpec((count, half), lambda i, c: (0, 1 - c[0]))
+    own, send = windowed(state_body, core, (key_rows, value_rows), [all_cols] * 2, [flat_state] * 2)
+    total = own + lax.ppermute(send, "core", swap)
+    mine_states = exchange(total)
+    sent = windowed(send_body, core, args, [away_cols] * 4, [sds((4, count, half), F32)])[0]
     got = lax.ppermute(sent, "core", swap)
-    qg, kv, total = call("state", state_body, core, (*args, got), [pair, pair, flat_state])
-    mine_states = exchange(total)
-    intra, my_gain = call(
-        "local", local_body, core, (qg, kv, gains), [act, sds((1, half), F32)]
-    )
-    sums = call(
-        "earlier", functools.partial(earlier_body, chips), core, (mine_states,), [flat_state]
-    )[0]
+    qg, kv = windowed(
+        place_body, core,
+        (*args, got), [my_cols] * 4 + [pl.BlockSpec(got.shape, lambda i, c: (0, 0, 0))],
+        [pair, pair],
+    )
+    intra, my_gain = call(local_body, core, (qg, kv, gains), [act, sds((1, half), F32)])
+    sums = call(functools.partial(earlier_body, chips), core, (mine_states, qg), [flat_state])[0]
     prior = exchange(sums)
     flat, parts = call(
-        "attn", attn_body, core, (qg, intra, prior, my_gain),
+        attn_body, core, (qg, intra, prior, my_gain),
         [act, sds((2 * columns, 4, DH), F32)],
     )
     parts = lax.all_to_all(parts, ("core", "head"), split_axis=0, concat_axis=0, tiled=True)
     gd, block = call(
-        "grad", functools.partial(grad_body, chips, full), core, (qg, flat, my_gain, parts),
+        functools.partial(grad_body, chips, full), core, (qg, flat, my_gain, parts),
         [act, padded],
     )
     mine_grads = exchange(block)
     keepq, keep, send = call(
-        "query", query_body, core, (qg, kv, gd, prior),
+        query_body, core, (qg, kv, gd, prior),
         [sds((count, half), BF16), sds((2, count, half), F32), sds((3, count, half), F32)],
         scratch=[pltpu.VMEM((3, both, half), F32)],
     )
     early = lax.ppermute(send, "core", swap)
-    later_sums = call(
-        "later", functools.partial(later_body, chips), core, (mine_grads,), [padded]
-    )[0]
+    later_sums = call(functools.partial(later_body, chips), core, (mine_grads,), [padded])[0]
     later = exchange(later_sums)
     others = lax.ppermute(later, "core", swap)
     gq, gk, gv, gain = call(
-        "final", functools.partial(final_body, chips), core,
+        functools.partial(final_body, chips), core,
         (key_rows, value_rows, keepq, keep, early, later, others),
         [sds((count, width), BF16)] * 3 + [sds((1, width), F32)], far=(7, 8, 9, 10),
     )

time: 106 us -> 109 us (1.028)
  blocking collectives: 51.2 us -> 32.5 us
  starting transfers between devices: 27.5 us -> 37 us
  waiting for transfers between devices: 15.6 us -> 24.3 us
  Pallas kernels: 10.1 us -> 12.5 us
    all_to_all x2 -> x1, blocking collectives: 33.9 us -> 15 us  [exchange(): lax.all_to_all(x.reshape(chips, 1, -1), 'chip', split_axis=0, concat_axis...]
    all_to_all x2 -> x3, waiting for transfers between devices: 12.2 us -> 21.7 us  [exchange(): lax.all_to_all(x.reshape(chips, 1, -1), 'chip', split_axis=0, concat_axis...]
    all_to_all x2 -> x3, starting transfers between devices: 9.27 us -> 16.9 us  [exchange(): lax.all_to_all(x.reshape(chips, 1, -1), 'chip', split_axis=0, concat_axis...]
    pallas_call x9 -> x10, Pallas kernels: 10.1 us -> 12.5 us  [the longest x7 8.42 us: call(): pl.pallas_call(body, out_shape=outs, in_specs=[pl.BlockSpec(memory_space=...]
    ppermute x1, waiting for transfers between devices: 2.26 us -> 0.01 us  [shards(): got = lax.ppermute(sent, 'core', swap)]
    ppermute x0 -> x1, starting transfers between devices: none -> 1.92 us  [shards(): total = own + lax.ppermute(send, 'core', swap)]
    ppermute x0 -> x1, waiting for transfers between devices: none -> 1.5 us  [shards(): total = own + lax.ppermute(send, 'core', swap)]
  transfers between devices with their start and end apart: 5 -> 7, of which waited for: 4 -> 5; matrix products, arithmetic and copies ran while one was open for 0% -> 1% of each run, Pallas kernels for 4% -> 7%
where the time goes in v4:
time: 109 us
  starting transfers between devices  37 us (34%)
  blocking collectives  32.5 us (30%)
  waiting for transfers between devices  24.3 us (22%)
  Pallas kernels  12.5 us (11%)
    all_to_all x3, waiting for transfers between devices, exchange(): lax.all_to_all(x.reshape(chips, 1, -1), 'chip', split_axis=0, concat_axis...  21.7 us
    all_to_all x1, blocking collectives, shards(): lax.all_to_all(parts, ('core', 'head'), split_axis=0, concat_axis=0, tile...  17.4 us
    all_to_all x3, starting transfers between devices, exchange(): lax.all_to_all(x.reshape(chips, 1, -1), 'chip', split_axis=0, concat_axis...  16.9 us
    all_to_all x1, blocking collectives, exchange(): lax.all_to_all(x.reshape(chips, 1, -1), 'chip', split_axis=0, concat_axis...  15 us
    ppermute x1, starting transfers between devices, shards(): got = lax.ppermute(sent, 'core', swap)  8.75 us
    pallas_call x7, Pallas kernels, call(): pl.pallas_call(body, out_shape=outs, in_specs=[pl.BlockSpec(memory_space=...  8.42 us
    ppermute x1, starting transfers between devices, shards(): others = lax.ppermute(later, 'core', swap)  5.82 us
    pallas_call x3, Pallas kernels, windowed(): pl.pallas_call(body, out_shape=[pltpu.VMEM(o.shape, o.dtype) for o in out...  4.06 us
  transfers between devices with their start and end apart: 7, of which 5 were waited for; matrix products, arithmetic and copies ran while one was open for 1% of the time, Pallas kernels for 7%

profile of v4, /device:TPU:1, one launch (start us, length us, event | category | flops | bytes accessed | tf_op | source)
XLA Modules:
  0.0 108.8 jit_solution(7399957493594470320)
XLA Ops:
  0.6 1.2 %shard_map.84 = f32[4,128,512]{2,1,0:T(8,128)S(1)} custom-call(s32[1]{0:T(128)} %bitcast.c, bf16[128,1024]{1,0:T(8,128)(2,1)} %q.3, bf16[128,1024]{1,0:T(8,128)(2,1)} %k.7, bf16[128,1024]{1,0:T(8,128)(2,1)} %v.7, bf16[128,1024]{1,0:T(8,128)(2,1)} %g.3), custom_call_target="tpu_custom_call" | custom-call | tf_op jit(solution)/shard_map/pallas_call | solution.py:61
  1.8 8.7 %collective-permute-start = (f32[4,128,512]{2,1,0:T(8,128)S(1)}, f32[4,128,512]{2,1,0:T(8,128)S(1)}, u32[]{:S(2)}, u32[]{:S(2)}) collective-permute-start(f32[4,128,512]{2,1,0:T(8,128)S(1)} %shard_map.84), channel_id=1, source_target_pairs={{0,8},{8,0},{1,9},{9,1},{2,10},{10,2},{3,11},{11,3},{4,12},{12,4},... | collective-permute-start | bytes 3145736 | tf_op jit(solution)/shard_map/ppermute | solution.py:289
  10.6 1.3 %shard_map.87 = (f32[512,128]{1,0:T(8,128)S(1)}, f32[512,128]{1,0:T(8,128)S(1)}) custom-call(s32[1]{0:T(128)} %bitcast.c, bf16[128,1024]{1,0:T(8,128)(2,1)} %k.7, bf16[128,1024]{1,0:T(8,128)(2,1)} %v.7), custom_call_target="tpu_custom_call" | custom-call | tf_op jit(solution)/shard_map/pallas_call | solution.py:61
  11.9 1.9 %collective-permute-start.1 = (f32[512,128]{1,0:T(8,128)S(1)}, f32[512,128]{1,0:T(8,128)S(1)}, u32[]{:S(2)}, u32[]{:S(2)}) collective-permute-start(f32[512,128]{1,0:T(8,128)S(1)} %get-tuple-element.25), channel_id=1, source_target_pairs={{0,8},{8,0},{1,9},{9,1},{2,10},{10,2},{3,11},{11,3},{4,12},{12,4},... | collective-permute-start | bytes 786440 | tf_op jit(solution)/shard_map/ppermute | solution.py:286
  13.8 1.5 %collective-permute-done.1 = f32[512,128]{1,0:T(8,128)S(1)} collective-permute-done((f32[512,128]{1,0:T(8,128)S(1)}, f32[512,128]{1,0:T(8,128)S(1)}, u32[]{:S(2)}, u32[]{:S(2)}) %collective-permute-start.1) | collective-permute-done | bytes 262176 | tf_op jit(solution)/shard_map/ppermute | solution.py:286
  15.3 0.7 add.3
  16.0 7.5 %all-to-all-start = ((f32[32,1,2048]{2,1,0:T(1,128)}), f32[32,1,2048]{2,1,0:T(1,128)S(1)}, u32[]{:S(2)}, u32[]{:S(2)}) async-start(f32[32,1,2048]{2,1,0:T(1,128)} %bitcast.2), calls=%async_computation | async-start | bytes 524288 | tf_op jit(solution)/shard_map/all_to_all | solution.py:277
  23.6 1.0 copy-done.3
  24.6 1.6 %shard_map.85 = (bf16[2,256,512]{2,1,0:T(8,128)(2,1)S(1)}, bf16[2,256,512]{2,1,0:T(8,128)(2,1)S(1)}) custom-call(s32[1]{0:T(128)} %bitcast.c, bf16[128,1024]{1,0:T(8,128)(2,1)} %q.3, bf16[128,1024]{1,0:T(8,128)(2,1)} %k.7, bf16[128,1024]{1,0:T(8,128)(2,1)} %v.7, bf16[128,1024]{1,0:T(8,128)(2,1)} %g.3, f32[4,128,512]{2,1,0:T(8,128)} %copy-done.3), custom_call_target="tpu_custom_call" | custom-call | tf_op jit(solution)/shard_map/pallas_call | solution.py:61
  26.2 9.1 %all-to-all-done = f32[32,1,2048]{2,1,0:T(1,128)S(1)} async-done(((f32[32,1,2048]{2,1,0:T(1,128)}), f32[32,1,2048]{2,1,0:T(1,128)S(1)}, u32[]{:S(2)}, u32[]{:S(2)}) %all-to-all-start) | async-done | bytes 262176 | tf_op jit(solution)/shard_map/all_to_all | solution.py:277
  35.2 0.7 shard_map.88
  36.0 4.7 %all-to-all-start.1 = ((f32[32,1,2048]{2,1,0:T(1,128)}), f32[32,1,2048]{2,1,0:T(1,128)S(1)}, u32[]{:S(2)}, u32[]{:S(2)}) async-start(f32[32,1,2048]{2,1,0:T(1,128)} %bitcast.4), calls=%async_computation.1 | async-start | bytes 524288 | tf_op jit(solution)/shard_map/all_to_all | solution.py:277
  40.7 1.4 %shard_map.86 = (f32[256,512]{1,0:T(8,128)S(1)}, f32[1,512]{1,0:T(1,128)S(1)}) custom-call(s32[1]{0:T(128)} %bitcast.c, bf16[2,256,512]{2,1,0:T(8,128)(2,1)S(1)} %get-tuple-element.21.qg.after, bf16[2,256,512]{2,1,0:T(8,128)(2,1)S(1)} %get-tuple-element.22.kv, f32[1,1024]{1,0:T(1,128)S(1)} %bitcast.18), custom_call_target="tpu_custom_call" | custom-call | tf_op jit(solution)/shard_map/pallas_call | solution.py:50
  42.0 9.0 %all-to-all-done.1 = f32[32,1,2048]{2,1,0:T(1,128)S(1)} async-done(((f32[32,1,2048]{2,1,0:T(1,128)}), f32[32,1,2048]{2,1,0:T(1,128)S(1)}, u32[]{:S(2)}, u32[]{:S(2)}) %all-to-all-start.1) | async-done | bytes 262176 | tf_op jit(solution)/shard_map/all_to_all | solution.py:277
  51.5 17.4 %all_to_all.25.parts = f32[16,4,128]{2,1,0:T(4,128)S(1)} all-to-all(f32[16,4,128]{2,1,0:T(4,128)S(1)} %get-tuple-element.28), channel_id=1, replica_groups=mesh['chip'=32,'core'=2,'head'=8] {'core','head'}, dimensions={0} | all-to-all | bytes 65536 | tf_op jit(solution)/shard_map/all_to_all | solution.py:302
  69.5 15.0 %all_to_all.26 = f32[32,1,2176]{2,1,0:T(1,128)S(1)} all-to-all(f32[32,1,2176]{2,1,0:T(1,128)S(1)} %bitcast.17), channel_id=1, replica_groups=mesh['chip'=32,'core'=2,'head'=8] {'chip'}, dimensions={0} | all-to-all | bytes 557056 | tf_op jit(solution)/shard_map/all_to_all | solution.py:277
  84.5 0.7 shard_map.92
  85.2 4.7 %all-to-all-start.4 = ((f32[32,1,2176]{2,1,0:T(1,128)}), f32[32,1,2176]{2,1,0:T(1,128)S(1)}, u32[]{:S(2)}, u32[]{:S(2)}) async-start(f32[32,1,2176]{2,1,0:T(1,128)} %bitcast.8), calls=%async_computation.4 | async-start | bytes 557056 | tf_op jit(solution)/shard_map/all_to_all | solution.py:277
  89.9 3.3 %shard_map.91 = (bf16[128,512]{1,0:T(8,128)(2,1)S(1)}, f32[2,128,512]{2,1,0:T(8,128)S(1)}, f32[3,128,512]{2,1,0:T(8,128)}) custom-call(s32[1]{0:T(128)} %bitcast.c, bf16[2,256,512]{2,1,0:T(8,128)(2,1)S(1)} %get-tuple-element.21.qg.after, bf16[2,256,512]{2,1,0:T(8,128)(2,1)S(1)} %get-tuple-element.22.kv, f32[256,512]{1,0:T(8,128)S(1)} %get-tuple-element.29.gd, ...), custom_call_target="tpu_custom_call" | custom-call | tf_op jit(solution)/shard_map/pallas_call | solution.py:50
  93.2 3.7 %collective-permute-start.2 = (f32[3,128,512]{2,1,0:T(8,128)}, f32[3,128,512]{2,1,0:T(8,128)S(1)}, u32[]{:S(2)}, u32[]{:S(2)}) collective-permute-start(f32[3,128,512]{2,1,0:T(8,128)} %get-tuple-element.32), channel_id=1, source_target_pairs={{0,8},{8,0},{1,9},{9,1},{2,10},{10,2},{3,11},{11,3},{4,12},{12,4},... | collective-permute-start | bytes 2359304 | tf_op jit(solution)/shard_map/ppermute | solution.py:313
  96.9 3.6 %all-to-all-done.4 = f32[32,1,2176]{2,1,0:T(1,128)S(1)} async-done(((f32[32,1,2176]{2,1,0:T(1,128)}), f32[32,1,2176]{2,1,0:T(1,128)S(1)}, u32[]{:S(2)}, u32[]{:S(2)}) %all-to-all-start.4) | async-done | bytes 278560 | tf_op jit(solution)/shard_map/all_to_all | solution.py:277
  100.4 5.8 %collective-permute-start.3 = (f32[544,128]{1,0:T(8,128)S(1)}, f32[544,128]{1,0:T(8,128)S(1)}, u32[]{:S(2)}, u32[]{:S(2)}) collective-permute-start(f32[544,128]{1,0:T(8,128)S(1)} %bitcast.14), channel_id=1, source_target_pairs={{0,8},{8,0},{1,9},{9,1},{2,10},{10,2},{3,11},{11,3},{4,12},{12,4},... | collective-permute-start | bytes 835592 | tf_op jit(solution)/shard_map/ppermute | solution.py:316
  106.3 1.2 %collective-permute-done.3.other = f32[544,128]{1,0:T(8,128)S(1)} collective-permute-done((f32[544,128]{1,0:T(8,128)S(1)}, f32[544,128]{1,0:T(8,128)S(1)}, u32[]{:S(2)}, u32[]{:S(2)}) %collective-permute-start.3) | collective-permute-done | bytes 278560 | tf_op jit(solution)/shard_map/ppermute | solution.py:316
  107.4 1.3 %shard_map.93 = (bf16[128,1024]{1,0:T(8,128)(2,1)}, bf16[128,1024]{1,0:T(8,128)(2,1)}, bf16[128,1024]{1,0:T(8,128)(2,1)}, f32[1,1024]{1,0:T(1,128)}) custom-call(s32[1]{0:T(128)} %bitcast.c, bf16[128,1024]{1,0:T(8,128)(2,1)S(1)} %copy-done, bf16[128,1024]{1,0:T(8,128)(2,1)S(1)} %copy-done.1, bf16[128,512]{1,0:T(8,128)(2,1)S(1)} %get-tuple-element.30.keepq, ...), custom_call_target="tpu_custom_call" | custom-call | tf_op jit(solution)/shard_map/pallas_call | solution.py:50
  (11 shorter events, 0.9 us)
Async XLA Ops:
  1.8 21.8 %collective-permute-start = (f32[4,128,512]{2,1,0:T(8,128)S(1)}, f32[4,128,512]{2,1,0:T(8,128)S(1)}, u32[]{:S(2)}, u32[]{:S(2)}) collective-permute-start(f32[4,128,512]{2,1,0:T(8,128)S(1)} %shard_map.84), channel_id=1, source_target_pairs={{0,8},{8,0},{1,9},{9,1},{2,10},{10,2},{3,11},{11,3},{4,12},{12,4},... | collective-permute-start | bytes 3145736 | tf_op jit(solution)/shard_map/ppermute | solution.py:289
  11.9 3.4 %collective-permute-start.1 = (f32[512,128]{1,0:T(8,128)S(1)}, f32[512,128]{1,0:T(8,128)S(1)}, u32[]{:S(2)}, u32[]{:S(2)}) collective-permute-start(f32[512,128]{1,0:T(8,128)S(1)} %get-tuple-element.25), channel_id=1, source_target_pairs={{0,8},{8,0},{1,9},{9,1},{2,10},{10,2},{3,11},{11,3},{4,12},{12,4},... | collective-permute-start | bytes 786440 | tf_op jit(solution)/shard_map/ppermute | solution.py:286
  16.0 19.2 %all-to-all-start = ((f32[32,1,2048]{2,1,0:T(1,128)}), f32[32,1,2048]{2,1,0:T(1,128)S(1)}, u32[]{:S(2)}, u32[]{:S(2)}) async-start(f32[32,1,2048]{2,1,0:T(1,128)} %bitcast.2), calls=%async_computation | async-start | bytes 524288 | tf_op jit(solution)/shard_map/all_to_all | solution.py:277
  23.6 1.0 copy-start.3
  36.0 4.7 %copy-start.2 = (f32[1024]{0:T(1024)S(1)}, f32[1024]{0:T(1024)}, u32[]{:S(2)}) copy-start(f32[1024]{0:T(1024)} %param.9) | copy-start | bytes 12292
  36.0 15.1 %all-to-all-start.1 = ((f32[32,1,2048]{2,1,0:T(1,128)}), f32[32,1,2048]{2,1,0:T(1,128)S(1)}, u32[]{:S(2)}, u32[]{:S(2)}) async-start(f32[32,1,2048]{2,1,0:T(1,128)} %bitcast.4), calls=%async_computation.1 | async-start | bytes 524288 | tf_op jit(solution)/shard_map/all_to_all | solution.py:277
  85.2 15.2 %all-to-all-start.4 = ((f32[32,1,2176]{2,1,0:T(1,128)}), f32[32,1,2176]{2,1,0:T(1,128)S(1)}, u32[]{:S(2)}, u32[]{:S(2)}) async-start(f32[32,1,2176]{2,1,0:T(1,128)} %bitcast.8), calls=%async_computation.4 | async-start | bytes 557056 | tf_op jit(solution)/shard_map/all_to_all | solution.py:277
  89.9 17.6 %copy-start = (bf16[128,1024]{1,0:T(8,128)(2,1)S(1)}, bf16[128,1024]{1,0:T(8,128)(2,1)}, u32[]{:S(2)}) copy-start(bf16[128,1024]{1,0:T(8,128)(2,1)} %k.7) | copy-start | bytes 786436
  89.9 17.5 %copy-start.1 = (bf16[128,1024]{1,0:T(8,128)(2,1)S(1)}, bf16[128,1024]{1,0:T(8,128)(2,1)}, u32[]{:S(2)}) copy-start(bf16[128,1024]{1,0:T(8,128)(2,1)} %v.7) | copy-start | bytes 786436
  93.2 13.1 %collective-permute-start.2 = (f32[3,128,512]{2,1,0:T(8,128)}, f32[3,128,512]{2,1,0:T(8,128)S(1)}, u32[]{:S(2)}, u32[]{:S(2)}) collective-permute-start(f32[3,128,512]{2,1,0:T(8,128)} %get-tuple-element.32), channel_id=1, source_target_pairs={{0,8},{8,0},{1,9},{9,1},{2,10},{10,2},{3,11},{11,3},{4,12},{12,4},... | collective-permute-start | bytes 2359304 | tf_op jit(solution)/shard_map/ppermute | solution.py:313
  100.4 7.0 %collective-permute-start.3 = (f32[544,128]{1,0:T(8,128)S(1)}, f32[544,128]{1,0:T(8,128)S(1)}, u32[]{:S(2)}, u32[]{:S(2)}) collective-permute-start(f32[544,128]{1,0:T(8,128)S(1)} %bitcast.14), channel_id=1, source_target_pairs={{0,8},{8,0},{1,9},{9,1},{2,10},{10,2},{3,11},{11,3},{4,12},{12,4},... | collective-permute-start | bytes 835592 | tf_op jit(solution)/shard_map/ppermute | solution.py:316
